TPU v7x, 256 devices: a whole 4x4x8 slice. The times are simulated.
256 devices in a mesh: ha: 16 (over x, y_hi, core), wa: 16 (over z, y_lo).
Axes of the slice: x: 4, y: 4 (y_hi: 2, y_lo: 2; y = y_hi * 2 + y_lo), z: 8, core: 2. Of those that a mesh axis runs over, the one named last changes fastest.
Arguments:
- tokens: bfloat16 [256, 256, 256], P('ha', 'wa'), may hold values from -6 to 6
- gain_attn: float32 [256], replicated, may hold values from 0.25 to 1.75
- qkv_fine: bfloat16 [256, 768], replicated, may hold values from -0.375 to 0.375
- scale_fine: float32 [4], replicated, may hold values from 2 to 24
- out_fine: bfloat16 [256, 256], replicated, may hold values from -0.375 to 0.375
- gain_ffn: float32 [256], replicated, may hold values from 0.25 to 1.75
- ffn_in: bfloat16 [256, 1536], replicated, may hold values from -0.375 to 0.375
- ffn_out: bfloat16 [768, 256], replicated, may hold values from -0.21875 to 0.21875
- up_proj: bfloat16 [256, 1024], replicated, may hold values from -0.375 to 0.375
- gain_coarse: float32 [1024], replicated, may hold values from 0.25 to 1.75
- qkv_coarse: bfloat16 [1024, 3072], replicated, may hold values from -0.1875 to 0.1875
- scale_coarse: float32 [16], replicated, may hold values from 2 to 24
- out_coarse: bfloat16 [1024, 1024], replicated, may hold values from -0.1875 to 0.1875
Outputs:
- fine_out: bfloat16 [256, 256, 256], P('ha', 'wa')
- coarse_out: bfloat16 [16, 16, 1024], P('ha', 'wa')
All inputs are finite; a program needn't handle non-finite values.
Results may differ from a plain program's by a relative error of at most 0.03.
Values may be sent and summed in bfloat16 or wider, within the bound.
A program may use at most 128 MiB of HBM per device.

v0:
```python
import jax
import jax.numpy as jnp
from jax import lax
from jax.sharding import PartitionSpec as P

CC = 1024
HD = 64
FFH = 768
RADIUS = 3
POOL = 16


def with_halo(cells, sides, width):
    for axis, dim in sides:
        count = lax.axis_size(axis)
        ends = count - 1
        head = lax.slice_in_dim(cells, 0, width, axis=dim)
        tail = lax.slice_in_dim(cells, cells.shape[dim] - width, cells.shape[dim], axis=dim)
        cells = jnp.concatenate(
            [
                lax.ppermute(tail, axis, [(i, (i + 1) % count) for i in range(ends)]),
                cells,
                lax.ppermute(head, axis, [((i + 1) % count, i) for i in range(ends)]),
            ],
            axis=dim,
        )
    return cells


def rms_scale(values, gain):
    values = values.astype(jnp.float32)
    return values * lax.rsqrt(jnp.mean(values * values, -1, keepdims=True) + 1e-06) * gain


def head_norm(values, heads):
    shaped = values.reshape(values.shape[:-1] + (heads, HD))
    return shaped * lax.rsqrt(jnp.mean(shaped * shaped, -1, keepdims=True) + 1e-06)


def attend_all(queries, keys_all, values_all, scales):
    cscores = (
        jnp.einsum("qhd,khd->hqk", queries, keys_all, preferred_element_type=jnp.float32)
        * (scales / HD)[:, None, None]
    )
    ctop = jnp.max(cscores, -1, keepdims=True)
    cexp = jnp.exp(cscores - ctop)
    cweights = (cexp / jnp.sum(cexp, -1, keepdims=True)).astype(jnp.bfloat16)
    return jnp.einsum(
        "hqk,khd->qhd", cweights, values_all, preferred_element_type=jnp.float32
    ).astype(jnp.bfloat16)


def shards(
    tokens,
    gain_attn,
    qkv_fine,
    scale_fine,
    out_fine,
    gain_ffn,
    ffn_in,
    ffn_out,
    up_proj,
    gain_coarse,
    qkv_coarse,
    scale_coarse,
    out_coarse,
):
    rows, cols, width = tokens.shape
    heads = width // HD
    count = rows * cols
    normed = rms_scale(tokens, gain_attn).astype(jnp.bfloat16).reshape(count, width)
    proj = jnp.dot(normed, qkv_fine, preferred_element_type=jnp.float32).reshape(
        rows, cols, 3 * width
    )
    query = head_norm(proj[..., :width], heads).astype(jnp.bfloat16).reshape(count, heads, HD)
    key_flat = head_norm(proj[..., width : 2 * width], heads).reshape(rows, cols, width)
    pairs = jnp.concatenate([key_flat, proj[..., 2 * width :]], -1).astype(jnp.bfloat16)
    padded = with_halo(pairs, (("ha", 0), ("wa", 1)), RADIUS)
    row_ids = lax.axis_index("ha") * rows + jnp.arange(rows + 2 * RADIUS, dtype=jnp.int32) - RADIUS
    col_ids = lax.axis_index("wa") * cols + jnp.arange(cols + 2 * RADIUS, dtype=jnp.int32) - RADIUS
    row_ok = (row_ids >= 0) & (row_ids < rows * lax.axis_size("ha"))
    col_ok = (col_ids >= 0) & (col_ids < cols * lax.axis_size("wa"))
    valid = row_ok[:, None] & col_ok[None, :]
    span = 2 * RADIUS + 1
    key_list = []
    value_list = []
    valid_list = []
    for shift_a in range(span):
        for shift_b in range(span):
            window = padded[shift_a : shift_a + rows, shift_b : shift_b + cols]
            key_list.append(window[..., :width])
            value_list.append(window[..., width:])
            valid_list.append(valid[shift_a : shift_a + rows, shift_b : shift_b + cols])
    key_stack = jnp.stack(key_list).reshape(span * span, count, heads, HD)
    value_stack = jnp.stack(value_list).reshape(span * span, count, heads, HD)
    valid_stack = jnp.stack(valid_list).reshape(span * span, count)
    raw = (
        jnp.einsum("nhd,snhd->hsn", query, key_stack, preferred_element_type=jnp.float32)
        * (scale_fine / HD)[:, None, None]
    )
    scores = jnp.where(valid_stack[None], raw, -1e30)
    top = jnp.max(scores, 1, keepdims=True)
    expo = jnp.exp(scores - top)
    weights = (expo / jnp.sum(expo, 1, keepdims=True)).astype(jnp.bfloat16)
    attn = jnp.einsum("hsn,snhd->nhd", weights, value_stack, preferred_element_type=jnp.float32)
    attn = attn.astype(jnp.bfloat16).reshape(count, width)
    h1 = (
        tokens.reshape(count, width).astype(jnp.float32)
        + jnp.dot(attn, out_fine, preferred_element_type=jnp.float32)
    ).astype(jnp.bfloat16)
    n2 = rms_scale(h1, gain_ffn).astype(jnp.bfloat16)
    mixed = jnp.dot(n2, ffn_in, preferred_element_type=jnp.float32)
    gated = (jax.nn.gelu(mixed[:, :FFH], approximate=True) * mixed[:, FFH:]).astype(jnp.bfloat16)
    fine_out = (
        h1.astype(jnp.float32) + jnp.dot(gated, ffn_out, preferred_element_type=jnp.float32)
    ).astype(jnp.bfloat16)
    fine_out = fine_out.reshape(rows, cols, width)
    rows_c, cols_c = (rows // POOL, cols // POOL)
    pooled = (
        fine_out.astype(jnp.float32).reshape(rows_c, POOL, cols_c, POOL, width).mean(axis=(1, 3))
    )
    pooled = pooled.astype(jnp.bfloat16).reshape(rows_c * cols_c, width)
    heads_c = CC // HD
    coarse = jnp.dot(pooled, up_proj, preferred_element_type=jnp.float32).astype(jnp.bfloat16)
    ncoarse = rms_scale(coarse, gain_coarse).astype(jnp.bfloat16)
    pc = jnp.dot(ncoarse, qkv_coarse, preferred_element_type=jnp.float32)
    cq = head_norm(pc[:, :CC], heads_c).astype(jnp.bfloat16)
    local_kv = jnp.concatenate(
        [head_norm(pc[:, CC : 2 * CC], heads_c).reshape(-1, CC), pc[:, 2 * CC :]], -1
    ).astype(jnp.bfloat16)
    all_kv = lax.all_gather(local_kv, ("ha", "wa"), axis=0, tiled=True)
    ck = all_kv[:, :CC].reshape(-1, heads_c, HD)
    cv = all_kv[:, CC:].reshape(-1, heads_c, HD)
    cattn = attend_all(cq, ck, cv, scale_coarse).reshape(-1, CC)
    coarse_out = (
        coarse.astype(jnp.float32) + jnp.dot(cattn, out_coarse, preferred_element_type=jnp.float32)
    ).astype(jnp.bfloat16)
    return (fine_out, coarse_out.reshape(rows_c, cols_c, CC))


def solution(mesh):
    return jax.shard_map(
        shards,
        mesh=mesh,
        in_specs=(P("ha", "wa", None), P(), P(), P(), P(), P(), P(), P(), P(), P(), P(), P(), P()),
        out_specs=(P("ha", "wa", None), P("ha", "wa", None)),
        check_vma=False,
    )
```

profile of v0, /device:TPU:1, one launch (start us, length us, event | category | flops | bytes accessed | tf_op | source)
XLA Modules:
  0.0 1165.6 jit_solution(1315303001375330019)
XLA Ops:
  13.5 2.1 mul.205
  17.9 5.1 collective-permute-start.1
  23.0 3.0 collective-permute-start
  71.0 5.1 collective-permute-start.2
  114.0 1.8 stack.509
  139.0 1.8 stack.526
  148.0 1.8 stack.532
  149.8 1.8 stack.533
  169.5 1.8 stack.546
  175.0 1.9 constant_dynamic-update-slice_fusion.47
  190.9 1.9 constant_dynamic-update-slice_fusion.38
  236.3 23.5 %fusion = f32[4,256,1,49]{3,2,1,0:T(1,128)} fusion(bf16[49,256,4,64]{3,2,1,0:T(4,128)(2,1)} %constant_dynamic-update-slice_fusion, bf16[256,4,64,1]{2,1,0,3:T(4,128)(2,1)S(1)} %copy-done.48), kind=kOutput, calls=%fused_computation.1 | convolution fusion | flops 6422528 | bytes 6754304 | tf_op jit(solution)/shard_map/nhd,snhd->hsn/dot_general | solution.py:98
  262.4 5.2 copy.36
  267.6 1.8 stack.550
  297.9 1.8 stack.569
  301.5 1.8 stack.571
  335.5 1.8 stack.593
  341.8 1.8 stack.598
  343.8 1.9 constant_dynamic-update-slice_fusion.96
  404.2 18.4 %multiply_reduce_fusion = bf16[256,4,64]{2,1,0:T(4,128)(2,1)S(1)} fusion(f32[256,4,49]{1,0,2:T(8,128)} %copy.36, bf16[49,256,4,64]{3,2,1,0:T(4,128)(2,1)} %constant_dynamic-update-slice_fusion.49), kind=kLoop, calls=%fused_computation | loop fusion | flops 9568256 | bytes 6754304
  424.7 2.1 convert_reduce_fusion
  428.3 3.7 fusion.60
  433.4 718.4 %all-gather.3.cloned.1.call-done = bf16[256,1,2048]{2,1,0:T(2,128)(2,1)} async-done(((bf16[1,1,2048]{2,1,0:T(2,128)(2,1)}), bf16[256,1,2048]{2,1,0:T(2,128)(2,1)}) %all-gather.3.cloned.1.call-update) | async-done | bytes 1048592 | tf_op jit(solution)/shard_map/all_gather | solution.py:131
  1151.8 2.2 copy.55
  (421 shorter events, 337.0 us)
Async XLA Ops:
  7.2 1150.2 %copy-start = (bf16[1024,1024]{1,0:T(8,128)(2,1)S(1)}, bf16[1024,1024]{1,0:T(8,128)(2,1)}, u32[]{:S(2)}) copy-start(bf16[1024,1024]{1,0:T(8,128)(2,1)} %param.25) | copy-start | bytes 6291460
  7.2 1144.6 %all-gather.3.cloned.1.call-start = ((), (), s32[]{:S(2)}) async-start(), calls=%async_computation | async-start | bytes 2105344 | tf_op jit(solution)/shard_map/all_gather | solution.py:131
  17.9 50.3 %collective-permute-start.1 = (bf16[3,16,512]{2,1,0:T(8,128)(2,1)}, bf16[3,16,512]{2,1,0:T(8,128)(2,1)}, u32[]{:S(2)}, u32[]{:S(2)}) collective-permute-start(bf16[3,16,512]{2,1,0:T(8,128)(2,1)} %get-tuple-element.113), channel_id=1, source_target_pairs={{16,0},{32,16},{48,32},{64,48},{80,64},{96,80},{112,96},{128,112},... | collective-permute-start | bytes 147464 | tf_op jit(solution)/shard_map/ppermute | solution.py:23
  23.0 45.2 %collective-permute-start = (bf16[3,16,512]{2,1,0:T(8,128)(2,1)}, bf16[3,16,512]{2,1,0:T(8,128)(2,1)}, u32[]{:S(2)}, u32[]{:S(2)}) collective-permute-start(bf16[3,16,512]{2,1,0:T(8,128)(2,1)} %get-tuple-element.112), channel_id=1, source_target_pairs={{0,16},{16,32},{32,48},{48,64},{64,80},{80,96},{96,112},{112,128},... | collective-permute-start | bytes 147464 | tf_op jit(solution)/shard_map/ppermute | solution.py:21
  69.7 21.1 %collective-permute-start.3 = (bf16[22,3,512]{2,1,0:T(4,128)(2,1)}, bf16[22,3,512]{2,1,0:T(4,128)(2,1)}, u32[]{:S(2)}, u32[]{:S(2)}) collective-permute-start(bf16[22,3,512]{2,1,0:T(4,128)(2,1)} %get-tuple-element.96), channel_id=1, source_target_pairs={{1,0},{2,1},{3,2},{4,3},{5,4},{6,5},{7,6},{8,7},{9,8},{10,9},{11,1... | collective-permute-start | bytes 202760 | tf_op jit(solution)/shard_map/ppermute | solution.py:23
  71.0 19.8 %collective-permute-start.2 = (bf16[22,3,512]{2,1,0:T(4,128)(2,1)}, bf16[22,3,512]{2,1,0:T(4,128)(2,1)}, u32[]{:S(2)}, u32[]{:S(2)}) collective-permute-start(bf16[22,3,512]{2,1,0:T(4,128)(2,1)} %get-tuple-element.97), channel_id=1, source_target_pairs={{0,1},{1,2},{2,3},{3,4},{4,5},{5,6},{6,7},{7,8},{8,9},{9,10},{10,1... | collective-permute-start | bytes 202760 | tf_op jit(solution)/shard_map/ppermute | solution.py:21
  114.0 101.5 %copy-start.3 = (bf16[1,256,4,64]{3,2,1,0:T(4,128)(2,1)S(1)}, bf16[1,256,4,64]{3,2,1,0:T(4,128)(2,1)}, u32[]{:S(2)}) copy-start(bf16[1,256,4,64]{3,2,1,0:T(4,128)(2,1)} %stack.524) | copy-start | bytes 393220
  174.9 54.3 %copy-start.23 = (bf16[1,256,4,64]{3,2,1,0:T(4,128)(2,1)S(1)}, bf16[1,256,4,64]{3,2,1,0:T(4,128)(2,1)}, u32[]{:S(2)}) copy-start(bf16[1,256,4,64]{3,2,1,0:T(4,128)(2,1)} %stack.540) | copy-start | bytes 393220
  174.9 55.0 %copy-start.21 = (bf16[1,256,4,64]{3,2,1,0:T(4,128)(2,1)S(1)}, bf16[1,256,4,64]{3,2,1,0:T(4,128)(2,1)}, u32[]{:S(2)}) copy-start(bf16[1,256,4,64]{3,2,1,0:T(4,128)(2,1)} %stack.541) | copy-start | bytes 393220
  175.0 55.8 %copy-start.19 = (bf16[1,256,4,64]{3,2,1,0:T(4,128)(2,1)S(1)}, bf16[1,256,4,64]{3,2,1,0:T(4,128)(2,1)}, u32[]{:S(2)}) copy-start(bf16[1,256,4,64]{3,2,1,0:T(4,128)(2,1)} %stack.542) | copy-start | bytes 393220
  175.0 56.6 %copy-start.17 = (bf16[1,256,4,64]{3,2,1,0:T(4,128)(2,1)S(1)}, bf16[1,256,4,64]{3,2,1,0:T(4,128)(2,1)}, u32[]{:S(2)}) copy-start(bf16[1,256,4,64]{3,2,1,0:T(4,128)(2,1)} %stack.543) | copy-start | bytes 393220
  175.0 57.4 %copy-start.15 = (bf16[1,256,4,64]{3,2,1,0:T(4,128)(2,1)S(1)}, bf16[1,256,4,64]{3,2,1,0:T(4,128)(2,1)}, u32[]{:S(2)}) copy-start(bf16[1,256,4,64]{3,2,1,0:T(4,128)(2,1)} %stack.544) | copy-start | bytes 393220
  175.0 58.2 %copy-start.4 = (bf16[1,256,4,64]{3,2,1,0:T(4,128)(2,1)S(1)}, bf16[1,256,4,64]{3,2,1,0:T(4,128)(2,1)}, u32[]{:S(2)}) copy-start(bf16[1,256,4,64]{3,2,1,0:T(4,128)(2,1)} %stack.545) | copy-start | bytes 393220
  175.0 59.0 %copy-start.12 = (bf16[1,256,4,64]{3,2,1,0:T(4,128)(2,1)S(1)}, bf16[1,256,4,64]{3,2,1,0:T(4,128)(2,1)}, u32[]{:S(2)}) copy-start(bf16[1,256,4,64]{3,2,1,0:T(4,128)(2,1)} %stack.546) | copy-start | bytes 393220
  175.0 59.8 %copy-start.10 = (bf16[1,256,4,64]{3,2,1,0:T(4,128)(2,1)S(1)}, bf16[1,256,4,64]{3,2,1,0:T(4,128)(2,1)}, u32[]{:S(2)}) copy-start(bf16[1,256,4,64]{3,2,1,0:T(4,128)(2,1)} %stack.547) | copy-start | bytes 393220
  175.0 60.5 %copy-start.7 = (bf16[1,256,4,64]{3,2,1,0:T(4,128)(2,1)S(1)}, bf16[1,256,4,64]{3,2,1,0:T(4,128)(2,1)}, u32[]{:S(2)}) copy-start(bf16[1,256,4,64]{3,2,1,0:T(4,128)(2,1)} %stack.548) | copy-start | bytes 393220
  175.0 61.3 %copy-start.48 = (bf16[256,4,64,1]{2,1,0,3:T(4,128)(2,1)S(1)}, bf16[256,4,64,1]{2,1,0,3:T(4,128)(2,1)}, u32[]{:S(2)}) copy-start(bf16[256,4,64,1]{2,1,0,3:T(4,128)(2,1)} %fusion.22) | copy-start | bytes 393220
  267.6 104.3 %copy-start.2 = (bf16[1,256,4,64]{3,2,1,0:T(4,128)(2,1)S(1)}, bf16[1,256,4,64]{3,2,1,0:T(4,128)(2,1)}, u32[]{:S(2)}) copy-start(bf16[1,256,4,64]{3,2,1,0:T(4,128)(2,1)} %stack.567) | copy-start | bytes 393220
  343.7 54.9 %copy-start.16 = (bf16[1,256,4,64]{3,2,1,0:T(4,128)(2,1)S(1)}, bf16[1,256,4,64]{3,2,1,0:T(4,128)(2,1)}, u32[]{:S(2)}) copy-start(bf16[1,256,4,64]{3,2,1,0:T(4,128)(2,1)} %stack.592) | copy-start | bytes 393220
  343.7 55.7 %copy-start.13 = (bf16[1,256,4,64]{3,2,1,0:T(4,128)(2,1)S(1)}, bf16[1,256,4,64]{3,2,1,0:T(4,128)(2,1)}, u32[]{:S(2)}) copy-start(bf16[1,256,4,64]{3,2,1,0:T(4,128)(2,1)} %stack.593) | copy-start | bytes 393220
  343.7 56.5 %copy-start.14 = (bf16[1,256,4,64]{3,2,1,0:T(4,128)(2,1)S(1)}, bf16[1,256,4,64]{3,2,1,0:T(4,128)(2,1)}, u32[]{:S(2)}) copy-start(bf16[1,256,4,64]{3,2,1,0:T(4,128)(2,1)} %stack.594) | copy-start | bytes 393220
  343.7 58.1 %copy-start.11 = (bf16[1,256,4,64]{3,2,1,0:T(4,128)(2,1)S(1)}, bf16[1,256,4,64]{3,2,1,0:T(4,128)(2,1)}, u32[]{:S(2)}) copy-start(bf16[1,256,4,64]{3,2,1,0:T(4,128)(2,1)} %stack.596) | copy-start | bytes 393220
  343.7 58.9 %copy-start.8 = (bf16[1,256,4,64]{3,2,1,0:T(4,128)(2,1)S(1)}, bf16[1,256,4,64]{3,2,1,0:T(4,128)(2,1)}, u32[]{:S(2)}) copy-start(bf16[1,256,4,64]{3,2,1,0:T(4,128)(2,1)} %stack.597) | copy-start | bytes 393220
  343.7 59.7 %copy-start.9 = (bf16[1,256,4,64]{3,2,1,0:T(4,128)(2,1)S(1)}, bf16[1,256,4,64]{3,2,1,0:T(4,128)(2,1)}, u32[]{:S(2)}) copy-start(bf16[1,256,4,64]{3,2,1,0:T(4,128)(2,1)} %stack.598) | copy-start | bytes 393220
  (35 other events, 1534.3 us)
Sparse Core Ops, SparseCore 0:
  433.2 718.5 all-gather.2
where the time goes:
time: 1180 us; the launch traced here: 1170 us
  waiting for transfers between devices  718 us (61%)
  local copies, waits for them, and re-layouts  349 us (30%)
  matrix products  34.6 us (3%)
  other arithmetic  33.1 us (3%)
  between operations  16 us (1%)
  starting transfers between devices  14.5 us (1%)
    all_gather x1, waiting for transfers between devices, shards(): all_kv = lax.all_gather(local_kv, ('ha', 'wa'), axis=0, tiled=True)  718 us
    unnamed x206, local copies, waits for them, and re-layouts  130 us
    another operation x50, local copies, waits for them, and re-layouts, shards(): key_stack = jnp.stack(key_list).reshape(span * span, count, heads, HD)  85.8 us
    another operation x50, local copies, waits for them, and re-layouts, shards(): value_stack = jnp.stack(value_list).reshape(span * span, count, heads, HD)  78.3 us
    another operation x50, local copies, waits for them, and re-layouts, shards(): valid_stack = jnp.stack(valid_list).reshape(span * span, count)  34.8 us
  transfers between devices with their start and end apart: 5, of which 1 were waited for; matrix products, arithmetic and copies ran while one was open for 5% of the time, Pallas kernels for 0%

commit v1 on v0

v1 whole, which is shorter than its diff:
```python
import functools

import jax
import jax.numpy as jnp
import numpy as np
from jax import lax
from jax.experimental import pallas as pl
from jax.experimental.pallas import tpu as pltpu
from jax.sharding import PartitionSpec as P

C = 256
CC = 1024
HD = 64
FFH = 768
RADIUS = 3
SIDE = 16
COUNT = SIDE * SIDE
HEADS = 4
HEADS_C = 16
EPS = 1e-06
LOG2E = 1.4426950408889634
MESH = pl.DeviceIdType.MESH
BF = jnp.bfloat16
F32 = jnp.float32

PIECES = (
    (-1, 0, 0, 48),
    (1, 0, 48, 48),
    (0, -1, 96, 48),
    (0, 1, 144, 48),
    (-1, -1, 192, 16),
    (-1, 1, 208, 16),
    (1, -1, 224, 16),
    (1, 1, 240, 16),
)


def tables():
    span = {-1: range(SIDE - RADIUS, SIDE), 0: range(SIDE), 1: range(RADIUS)}
    pick = np.zeros((COUNT, COUNT), np.float32)
    row = np.full((2 * COUNT,), -100, np.int64)
    col = np.full((2 * COUNT,), -100, np.int64)
    own = np.arange(COUNT)
    row[:COUNT], col[:COUNT] = own // SIDE, own % SIDE
    for side_r, side_c, first, _ in PIECES:
        at = first
        for r in span[side_r]:
            for c in span[side_c]:
                pick[at, r * SIDE + c] = 1
                row[COUNT + at] = r + SIDE * side_r
                col[COUNT + at] = c + SIDE * side_c
                at += 1
    near = (np.abs(row[None] - (own // SIDE)[:, None]) <= RADIUS) & (
        np.abs(col[None] - (own % SIDE)[:, None]) <= RADIUS
    )
    heads = (own[:, None] // HD) == (own[None] // HD)
    table = np.concatenate([pick, near, heads], 1).astype(np.float32)
    place = np.zeros((8, 2 * COUNT), np.int32)
    place[0], place[1] = row, col
    return table, place


def dot(a, b):
    return jnp.dot(a, b, preferred_element_type=F32)


def dot_t(a, b):
    return lax.dot_general(a, b, (((1,), (1,)), ((), ())), preferred_element_type=F32)


def split(values):
    high = values.astype(BF)
    return high, (values - high.astype(F32)).astype(BF)


def rms(values, gain):
    return values * lax.rsqrt(jnp.mean(values * values, -1, keepdims=True) + EPS) * gain


def kernel(
    sizes,
    tokens,
    gain_attn,
    qkv_fine,
    scale_fine,
    out_fine,
    gain_ffn,
    ffn_in,
    ffn_out,
    up_proj,
    gain_coarse,
    qkv_coarse,
    scale_coarse,
    out_coarse,
    table,
    place,
    fine_o,
    coarse_o,
    tok_v,
    ga_v,
    qkv_v,
    out_v,
    gf_v,
    fin_v,
    fout_v,
    up_v,
    gc_v,
    qkvc_v,
    outc_v,
    table_v,
    place_v,
    send_v,
    halo_v,
    fine_v,
    row_v,
    rows_v,
    tile_v,
    tiles_v,
    last_v,
    local_sem,
    halo_send,
    halo_recv,
    row_send,
    row_recv,
    tile_send,
    tile_recv,
):
    n_ha, n_wa = sizes
    n_x, n_z = n_ha // 4, n_wa // 2
    g_row, g_tile = n_z * 2, n_x * 4
    ha, wa = lax.axis_index("ha"), lax.axis_index("wa")
    core = lax.rem(ha, 2)
    x = lax.div(ha, 4)
    z = lax.div(wa, 2)
    y = lax.rem(lax.div(ha, 2), 2) * 2 + lax.rem(wa, 2)

    neighbours = []
    for side_r, side_c, _, _ in PIECES:
        neighbours.append((lax.rem(ha - side_r + n_ha, n_ha), lax.rem(wa - side_c + n_wa, n_wa)))
    row_peers = []
    for d in range(1, g_row):
        to_z = lax.rem(z + d // 2, n_z)
        to_core = lax.rem(core + d % 2, 2)
        row_peers.append((ha - core + to_core, wa - 2 * z + 2 * to_z))
    tile_peers = []
    for d in range(1, g_tile):
        to_x = lax.rem(x + d // 4, n_x)
        to_y = lax.rem(y + d % 4, 4)
        tile_peers.append((4 * to_x + 2 * lax.div(to_y, 2) + core, 2 * z + lax.rem(to_y, 2)))

    barrier = pltpu.get_barrier_semaphore()
    peers = neighbours + row_peers + tile_peers
    for peer in peers:
        pl.semaphore_signal(barrier, inc=1, device_id=peer, device_id_type=MESH)

    loads = {}
    for i, (name, src, dst) in enumerate(
        (
            ("tok", tokens, tok_v),
            ("ga", gain_attn, ga_v),
            ("table", table, table_v),
            ("place", place, place_v),
            ("qkv", qkv_fine, qkv_v),
            ("out", out_fine, out_v),
            ("gf", gain_ffn, gf_v),
            ("fin", ffn_in, fin_v),
            ("fout", ffn_out, fout_v),
            ("up", up_proj, up_v),
            ("gc", gain_coarse, gc_v),
            ("qkvc", qkv_coarse, qkvc_v),
            ("outc", out_coarse, outc_v),
        )
    ):
        loads[name] = pltpu.make_async_copy(src, dst, local_sem.at[i])
        loads[name].start()

    loads["tok"].wait()
    loads["ga"].wait()
    tok = tok_v[...].astype(F32)
    normed = rms(tok, ga_v[...]).astype(BF)
    loads["table"].wait()
    send_v[...] = dot(table_v[:, :COUNT], normed).astype(BF)

    loads["qkv"].wait()
    loads["place"].wait()
    lane_head = lax.broadcasted_iota(jnp.int32, (COUNT, C), 1) // HD
    same = table_v[:, 3 * COUNT : 4 * COUNT]

    def head_scale(values):
        high, low = split(values * values)
        return lax.rsqrt((dot(high, same) + dot(low, same)) * (1 / HD) + EPS)

    def head_norm(values):
        return (values * head_scale(values)).astype(BF)

    pl.semaphore_wait(barrier, len(peers))
    halos = []
    for i, (_, _, first, rows) in enumerate(PIECES):
        copy = pltpu.make_async_remote_copy(
            src_ref=send_v.at[pl.ds(first, rows)],
            dst_ref=halo_v.at[pl.ds(first, rows)],
            send_sem=halo_send.at[i],
            recv_sem=halo_recv.at[i],
            device_id=neighbours[i],
            device_id_type=MESH,
        )
        copy.start()
        halos.append(copy)

    proj = dot(normed, qkv_v[...])
    query = head_norm(proj[:, :C])
    queries = [jnp.where(lane_head == h, query, jnp.zeros_like(query)) for h in range(HEADS)]
    ones = jnp.ones((COUNT, C), BF)
    zero = jnp.zeros((COUNT, C), BF)

    key_row = place_v[0:1, :] + ha * SIDE
    key_col = place_v[1:2, :] + wa * SIDE
    inside = (
        (key_row >= 0) & (key_row < SIDE * n_ha) & (key_col >= 0) & (key_col < SIDE * n_wa)
    ).astype(F32)

    def attend(key, value, part):
        cols = slice(COUNT * (1 + part), COUNT * (2 + part))
        mask = table_v[:, cols].astype(F32) * inside[:, COUNT * part : COUNT * (part + 1)]
        weights, values = [], []
        for h in range(HEADS):
            raw = dot_t(queries[h], key) * (scale_fine[h] * (LOG2E / HD))
            weights.append((jnp.exp2(raw) * mask).astype(BF))
            here = lane_head == h
            values.append(
                jnp.concatenate([jnp.where(here, value, zero), jnp.where(here, ones, zero)], 1)
            )
        return dot(jnp.concatenate(weights, 1), jnp.concatenate(values, 0))

    total = attend(head_norm(proj[:, C : 2 * C]), proj[:, 2 * C :].astype(BF), 0)

    for copy in halos:
        copy.wait_recv()
    proj_h = dot(halo_v[...], qkv_v[:, C:])
    total = total + attend(head_norm(proj_h[:, :C]), proj_h[:, C:].astype(BF), 1)
    attn = (total[:, :C] / total[:, C:]).astype(BF)

    loads["out"].wait()
    loads["gf"].wait()
    h1 = (tok_v[...].astype(F32) + dot(attn, out_v[...])).astype(BF)
    h1f = h1.astype(F32)
    n2 = rms(h1f, gf_v[...]).astype(BF)
    loads["fin"].wait()
    loads["fout"].wait()
    acc = h1f
    for part in range(FFH // C):
        cols = slice(part * C, (part + 1) * C)
        gate = dot(n2, fin_v[:, cols])
        lift = dot(n2, fin_v[:, FFH + part * C : FFH + (part + 1) * C])
        gated = (jax.nn.gelu(gate, approximate=True) * lift).astype(BF)
        acc = acc + dot(gated, fout_v[cols, :])
    fine = acc.astype(BF)
    pooled = jnp.mean(fine.astype(F32), 0, keepdims=True).astype(BF)

    rows_v[0] = pooled.astype(F32)
    row_v[...] = pooled.astype(F32)
    fine_v[...] = fine
    sends = []
    for d, peer in enumerate(row_peers, 1):
        copy = pltpu.make_async_remote_copy(
            src_ref=row_v,
            dst_ref=rows_v.at[d],
            send_sem=row_send.at[d],
            recv_sem=row_recv.at[d],
            device_id=peer,
            device_id_type=MESH,
        )
        copy.start()
        sends.append(copy)
    store = pltpu.make_async_copy(fine_v, fine_o, local_sem.at[13])
    store.start()

    loads["up"].wait()
    loads["gc"].wait()
    loads["qkvc"].wait()
    own = jnp.broadcast_to(pooled.astype(F32), (16, C)).astype(BF)
    coarse_own = dot(own, up_v[...]).astype(BF)
    nc_own = rms(coarse_own.astype(F32), gc_v[...]).astype(BF)
    cq = dot(nc_own, qkvc_v[:, :CC])
    head_of_row = lax.broadcasted_iota(jnp.int32, (HEADS_C, CC), 0)
    head_of_lane = lax.broadcasted_iota(jnp.int32, (HEADS_C, CC), 1) // HD
    diag = head_of_row == head_of_lane
    cq = jnp.where(diag, cq, 0.0)
    cq = cq * lax.rsqrt(jnp.sum(cq * cq, -1, keepdims=True) * (1 / HD) + EPS)
    cq = cq.astype(BF)
    head_sum = jnp.where(diag, 1.0, 0.0).astype(BF)
    scale_col = jnp.zeros((HEADS_C, 1), F32)
    row_id = lax.broadcasted_iota(jnp.int32, (HEADS_C, 1), 0)
    for h in range(HEADS_C):
        scale_col = jnp.where(row_id == h, scale_coarse[h] * (LOG2E / HD), scale_col)

    slot = lax.broadcasted_iota(jnp.int32, (g_row, C), 0)
    tile = jnp.zeros((g_row, C), F32)
    for copy in sends:
        copy.wait_recv()
    for d in range(g_row):
        tile = jnp.where(slot == d, rows_v[d], tile)
    tile_v[...] = tile.astype(BF)
    tiles_v[0] = tile.astype(BF)
    tiles = []
    for d, peer in enumerate(tile_peers, 1):
        copy = pltpu.make_async_remote_copy(
            src_ref=tile_v,
            dst_ref=tiles_v.at[d],
            send_sem=tile_send.at[d],
            recv_sem=tile_recv.at[d],
            device_id=peer,
            device_id_type=MESH,
        )
        copy.start()
        tiles.append(copy)
    for copy in tiles:
        copy.wait_recv()

    every = tiles_v[...].reshape(g_tile * g_row, C)
    coarse = dot(every, up_v[...]).astype(BF)
    nc = rms(coarse.astype(F32), gc_v[...]).astype(BF)
    ck = dot(nc, qkvc_v[:, CC : 2 * CC])
    high, low = split(ck * ck)
    size = (dot_t(head_sum, high) + dot_t(head_sum, low)) * (1 / HD)
    scores = dot_t(cq, ck.astype(BF)) * (lax.rsqrt(size + EPS) * scale_col)
    cexp = jnp.exp2(scores)
    cweights = (cexp / jnp.sum(cexp, -1, keepdims=True)).astype(BF)
    mixed = dot(cweights, nc).astype(BF)
    cattn = jnp.where(diag, dot(mixed, qkvc_v[:, 2 * CC :]), 0.0)
    cattn = jnp.sum(cattn, 0, keepdims=True)
    loads["outc"].wait()
    cattn = jnp.broadcast_to(cattn, (16, CC)).astype(BF)
    result = coarse_own.astype(F32) + dot(cattn, outc_v[...])
    last_v[...] = result[0:1].astype(BF)
    final = pltpu.make_async_copy(last_v, coarse_o, local_sem.at[14])
    final.start()

    for copy in halos + sends + tiles:
        copy.wait_send()
    store.wait()
    final.wait()


def solution(mesh):
    sizes = (mesh.shape["ha"], mesh.shape["wa"])
    g_row, g_tile = sizes[1], sizes[0]
    table, place = tables()
    table, place = jnp.asarray(table, BF), jnp.asarray(place)

    def shards(
        tokens,
        gain_attn,
        qkv_fine,
        scale_fine,
        out_fine,
        gain_ffn,
        ffn_in,
        ffn_out,
        up_proj,
        gain_coarse,
        qkv_coarse,
        scale_coarse,
        out_coarse,
    ):
        hbm = pl.BlockSpec(memory_space=pl.ANY)
        smem = pl.BlockSpec(memory_space=pltpu.SMEM)
        fine, coarse = pl.pallas_call(
            functools.partial(kernel, sizes),
            out_shape=(
                jax.ShapeDtypeStruct((COUNT, C), BF),
                jax.ShapeDtypeStruct((1, CC), BF),
            ),
            in_specs=[hbm, hbm, hbm, smem, hbm, hbm, hbm, hbm, hbm, hbm, hbm, smem, hbm, hbm, hbm],
            out_specs=(hbm, hbm),
            scratch_shapes=[
                pltpu.VMEM((COUNT, C), BF),
                pltpu.VMEM((1, C), F32),
                pltpu.VMEM((C, 3 * C), BF),
                pltpu.VMEM((C, C), BF),
                pltpu.VMEM((1, C), F32),
                pltpu.VMEM((C, 2 * FFH), BF),
                pltpu.VMEM((FFH, C), BF),
                pltpu.VMEM((C, CC), BF),
                pltpu.VMEM((1, CC), F32),
                pltpu.VMEM((CC, 3 * CC), BF),
                pltpu.VMEM((CC, CC), BF),
                pltpu.VMEM((COUNT, 4 * COUNT), BF),
                pltpu.VMEM((8, 2 * COUNT), jnp.int32),
                pltpu.VMEM((COUNT, C), BF),
                pltpu.VMEM((COUNT, C), BF),
                pltpu.VMEM((COUNT, C), BF),
                pltpu.VMEM((1, C), F32),
                pltpu.VMEM((g_row, 1, C), F32),
                pltpu.VMEM((g_row, C), BF),
                pltpu.VMEM((g_tile, g_row, C), BF),
                pltpu.VMEM((1, CC), BF),
                pltpu.SemaphoreType.DMA((15,)),
                pltpu.SemaphoreType.DMA((8,)),
                pltpu.SemaphoreType.DMA((8,)),
                pltpu.SemaphoreType.DMA((g_row,)),
                pltpu.SemaphoreType.DMA((g_row,)),
                pltpu.SemaphoreType.DMA((g_tile,)),
                pltpu.SemaphoreType.DMA((g_tile,)),
            ],
            compiler_params=pltpu.CompilerParams(
                collective_id=0, has_side_effects=True, vmem_limit_bytes=60 * 1024 * 1024
            ),
        )(
            tokens.reshape(COUNT, C),
            gain_attn.reshape(1, C),
            qkv_fine,
            scale_fine,
            out_fine,
            gain_ffn.reshape(1, C),
            ffn_in,
            ffn_out,
            up_proj,
            gain_coarse.reshape(1, CC),
            qkv_coarse,
            scale_coarse,
            out_coarse,
            table,
            place,
        )
        return fine.reshape(SIDE, SIDE, C), coarse.reshape(1, 1, CC)

    return jax.shard_map(
        shards,
        mesh=mesh,
        in_specs=(P("ha", "wa", None),) + (P(),) * 12,
        out_specs=(P("ha", "wa", None), P("ha", "wa", None)),
        check_vma=False,
    )
```

time: 1180 us -> 35.2 us (0.03); the launches traced: 1170 us -> 35 us
  waiting for transfers between devices: 718 us -> 0 us
  local copies, waits for them, and re-layouts: 349 us -> 2.85 us
  matrix products: 34.6 us -> 0 us
  other arithmetic: 33.1 us -> 0 us
  Pallas kernels: 0 us -> 31.5 us
  between operations: 16 us -> 0.64 us
  starting transfers between devices: 14.5 us -> 0 us
    all_gather x1 -> x0, waiting for transfers between devices: 718 us -> none  [shards(): all_kv = lax.all_gather(local_kv, ('ha', 'wa'), axis=0, tiled=True)]
    another operation x151 -> x0, local copies, waits for them, and re-layouts: 199 us -> none  [the longest x50 85.8 us: shards(): key_stack = jnp.stack(key_list).reshape(span * span, count, heads, HD)]
    unnamed x206 -> x2, local copies, waits for them, and re-layouts: 130 us -> 2.85 us
    dot_general x10 -> x0, matrix products: 34.6 us -> none  [the longest x1 23.5 us: shards(): jnp.einsum('nhd,snhd->hsn', query, key_stack, preferred_element_type=jnp....]
    pallas_call x0 -> x1, Pallas kernels: none -> 31.5 us  [shards(): pl.pallas_call(functools.partial(kernel, sizes), out_shape=(jax.ShapeDtyp...]
    unnamed x3 -> x0, other arithmetic: 19.9 us -> none
    ppermute x4 -> x0, starting transfers between devices: 14.5 us -> none  [the longest x2 8.13 us: with_halo(): lax.ppermute(tail, axis, [(i, (i + 1) % count) for i in range(ends)])]
    slice x14 -> x0, local copies, waits for them, and re-layouts: 11.8 us -> none  [the longest x5 7.28 us: shards(): value_list.append(window[..., width:])]
  transfers between devices with their start and end apart: 5 -> 0, of which waited for: 1 -> 0; matrix products, arithmetic and copies ran while one was open for 5% -> 0% of each run, Pallas kernels for 0% -> 0%
where the time goes in v1:
time: 35.2 us; the launch traced here: 35 us
  Pallas kernels  31.5 us (89%)
  local copies, waits for them, and re-layouts  2.85 us (8%)
  between operations  0.64 us (2%)
    pallas_call x1, Pallas kernels, shards(): pl.pallas_call(functools.partial(kernel, sizes), out_shape=(jax.ShapeDtyp...  31.5 us
    unnamed x2, local copies, waits for them, and re-layouts  2.85 us

profile of v1, /device:TPU:1, one launch (start us, length us, event | category | flops | bytes accessed | tf_op | source)
XLA Modules:
  0.0 35.0 jit_solution(14222541739693217050)
XLA Ops:
  0.6 31.5 %shard_map.158 = (bf16[256,256]{1,0:T(8,128)(2,1)}, bf16[1,1024]{1,0:T(2,128)(2,1)}) custom-call(bf16[256,256]{1,0:T(8,128)(2,1)} %bitcast.6, f32[1,256]{1,0:T(1,128)} %bitcast.10, bf16[256,768]{1,0:T(8,128)(2,1)} %qkv_fine.1, f32[4]{0:T(128)} %scale_fine.1, bf16[256,256]{1,0:T(8,128)(2,1)} %out_fine.1, f32[1,256]{1,0:T(1,128)} %bitcast.11, ...), custom_call_target="tpu_custom_call" | custom-call | tf_op jit(solution)/shard_map/pallas_call | solution.py:368
  32.2 1.6 %copy.19 = bf16[16,16,256]{2,1,0:T(8,128)(2,1)} copy(bf16[16,16,256]{2,1,0:T(8,128)(2,1)} %bitcast.7) | data formatting | bytes 262144
  33.7 1.3 %copy.20 = bf16[1,1,1024]{2,1,0:T(2,128)(2,1)} copy(bf16[1,1,1024]{2,1,0:T(2,128)(2,1)} %bitcast.9) | data formatting | bytes 4096

commit v2 on v1

v2 whole, which is shorter than its diff:
```python
import functools

import jax
import jax.numpy as jnp
import numpy as np
from jax import lax
from jax.experimental import pallas as pl
from jax.experimental.pallas import tpu as pltpu
from jax.sharding import PartitionSpec as P

C = 256
CC = 1024
HD = 64
FFH = 768
RADIUS = 3
SIDE = 16
COUNT = SIDE * SIDE
HEADS = 4
HEADS_C = 16
LANES = 128
EPS = 1e-06
VMEM = 40 * 1024 * 1024
LOG2E = 1.4426950408889634
MESH = pl.DeviceIdType.MESH
BF = jnp.bfloat16
F32 = jnp.float32

PIECES = (
    (-1, 0, 0, 48),
    (1, 0, 48, 48),
    (0, -1, 96, 48),
    (0, 1, 144, 48),
    (-1, -1, 192, 16),
    (-1, 1, 208, 16),
    (1, -1, 224, 16),
    (1, 1, 240, 16),
)


def tables():
    span = {-1: range(SIDE - RADIUS, SIDE), 0: range(SIDE), 1: range(RADIUS)}
    pick = np.zeros((COUNT, COUNT), np.float32)
    row = np.full((2 * COUNT,), -100, np.int64)
    col = np.full((2 * COUNT,), -100, np.int64)
    own = np.arange(COUNT)
    row[:COUNT], col[:COUNT] = own // SIDE, own % SIDE
    for side_r, side_c, first, _ in PIECES:
        at = first
        for r in span[side_r]:
            for c in span[side_c]:
                pick[at, r * SIDE + c] = 1
                row[COUNT + at] = r + SIDE * side_r
                col[COUNT + at] = c + SIDE * side_c
                at += 1
    near = (np.abs(row[None] - (own // SIDE)[:, None]) <= RADIUS) & (
        np.abs(col[None] - (own % SIDE)[:, None]) <= RADIUS
    )
    heads = (own[:, None] // HD) == (own[None] // HD)
    table = np.concatenate([pick, near, heads], 1).astype(np.float32)
    place = np.zeros((8, 2 * COUNT), np.int32)
    place[0], place[1] = row, col
    return table, place


def dot(a, b):
    return jnp.dot(a, b, preferred_element_type=F32)


def dot_t(a, b):
    return lax.dot_general(a, b, (((1,), (1,)), ((), ())), preferred_element_type=F32)


def split(values):
    high = values.astype(BF)
    return high, (values - high.astype(F32)).astype(BF)


def rms(values, gain):
    return values * lax.rsqrt(jnp.mean(values * values, -1, keepdims=True) + EPS) * gain


def kernel(
    sizes,
    tokens,
    gain_attn,
    qkv_fine,
    scale_fine,
    out_fine,
    gain_ffn,
    ffn_in,
    ffn_out,
    up_proj,
    gain_coarse,
    qkv_coarse,
    scale_coarse,
    out_coarse,
    table,
    place,
    fine_o,
    coarse_o,
    tok_v,
    ga_v,
    qkv_v,
    out_v,
    gf_v,
    fin_v,
    fout_v,
    up_v,
    gc_v,
    qkvc_v,
    outc_v,
    table_v,
    place_v,
    sf_s,
    sc_s,
    send_v,
    halo_v,
    row_v,
    rows_v,
    norm_v,
    norms_v,
    tile_v,
    tiles_v,
    ntile_v,
    ntiles_v,
    local_sem,
    halo_send,
    halo_recv,
    row_send,
    row_recv,
    norm_send,
    norm_recv,
    tile_send,
    tile_recv,
    ntile_send,
    ntile_recv,
):
    n_ha, n_wa = sizes
    n_x, n_z = n_ha // 4, n_wa // 2
    g_row, g_tile = n_z * 2, n_x * 4
    ha, wa = lax.axis_index("ha"), lax.axis_index("wa")
    core = lax.rem(ha, 2)
    x = lax.div(ha, 4)
    z = lax.div(wa, 2)
    y = lax.rem(lax.div(ha, 2), 2) * 2 + lax.rem(wa, 2)

    def far(step, count):
        return min(step, count - step)

    neighbours = []
    for side_r, side_c, _, _ in PIECES:
        neighbours.append((lax.rem(ha - side_r + n_ha, n_ha), lax.rem(wa - side_c + n_wa, n_wa)))
    barrier = pltpu.get_barrier_semaphore()
    for peer in neighbours:
        pl.semaphore_signal(barrier, inc=1, device_id=peer, device_id_type=MESH)

    names = ("tok", "ga", "table", "qkv", "place", "sf", "out", "gf", "fin", "fout")
    names += ("up", "gc", "sc", "qkvc", "outc")
    pairs = {
        "tok": (tokens, tok_v),
        "ga": (gain_attn, ga_v),
        "table": (table, table_v),
        "place": (place, place_v),
        "qkv": (qkv_fine, qkv_v),
        "sf": (scale_fine, sf_s),
        "out": (out_fine, out_v),
        "gf": (gain_ffn, gf_v),
        "fin": (ffn_in, fin_v),
        "fout": (ffn_out, fout_v),
        "up": (up_proj, up_v),
        "gc": (gain_coarse, gc_v),
        "sc": (scale_coarse, sc_s),
        "qkvc": (qkv_coarse, qkvc_v),
        "outc": (out_coarse, outc_v),
    }
    loads = {}
    for i, name in enumerate(names):
        loads[name] = pltpu.make_async_copy(*pairs[name], local_sem.at[i])
    for name in names[:6]:
        loads[name].start()

    row_peers = []
    for d in sorted(range(1, g_row), key=lambda d: -far(d // 2, n_z)):
        to_z = lax.rem(z + d // 2, n_z)
        to_core = lax.rem(core + d % 2, 2)
        row_peers.append((d, (ha - core + to_core, wa - 2 * z + 2 * to_z)))
    tile_peers = []
    for d in sorted(range(1, g_tile), key=lambda d: -far(d // 4, n_x) - far(d % 4, 4)):
        to_x = lax.rem(x + d // 4, n_x)
        to_y = lax.rem(y + d % 4, 4)
        peer = (4 * to_x + 2 * lax.div(to_y, 2) + core, 2 * z + lax.rem(to_y, 2))
        tile_peers.append((d, peer))
    for _, peer in row_peers + tile_peers:
        pl.semaphore_signal(barrier, inc=1, device_id=peer, device_id_type=MESH)
    for name in names[6:]:
        loads[name].start()

    def spread(src, dst, send_sem, recv_sem, peers):
        copies = []
        for d, peer in peers:
            copy = pltpu.make_async_remote_copy(
                src_ref=src,
                dst_ref=dst.at[d],
                send_sem=send_sem.at[d],
                recv_sem=recv_sem.at[d],
                device_id=peer,
                device_id_type=MESH,
            )
            copy.start()
            copies.append(copy)
        return copies

    loads["tok"].wait()
    loads["ga"].wait()
    tok = tok_v[...].astype(F32)
    normed = rms(tok, ga_v[...]).astype(BF)
    loads["table"].wait()
    send_v[...] = dot(table_v[:, :COUNT], normed).astype(BF)

    loads["qkv"].wait()
    loads["place"].wait()
    lane_head = lax.broadcasted_iota(jnp.int32, (COUNT, C), 1) // HD
    same = table_v[:, 3 * COUNT : 4 * COUNT]

    def head_scale(values):
        high, low = split(values * values)
        return lax.rsqrt((dot(high, same) + dot(low, same)) * (1 / HD) + EPS)

    def head_norm(values):
        return (values * head_scale(values)).astype(BF)

    pl.semaphore_wait(barrier, len(neighbours) + len(row_peers) + len(tile_peers))
    halos = []
    for i, (_, _, first, rows) in enumerate(PIECES):
        copy = pltpu.make_async_remote_copy(
            src_ref=send_v.at[pl.ds(first, rows)],
            dst_ref=halo_v.at[pl.ds(first, rows)],
            send_sem=halo_send.at[i],
            recv_sem=halo_recv.at[i],
            device_id=neighbours[i],
            device_id_type=MESH,
        )
        copy.start()
        halos.append(copy)

    proj = dot(normed, qkv_v[...])
    query = head_norm(proj[:, :C])
    queries = [jnp.where(lane_head == h, query, jnp.zeros_like(query)) for h in range(HEADS)]
    one, zero = jnp.ones((COUNT, C), BF), jnp.zeros((COUNT, C), BF)

    key_row = place_v[0:1, :] + ha * SIDE
    key_col = place_v[1:2, :] + wa * SIDE
    inside = (
        (key_row >= 0) & (key_row < SIDE * n_ha) & (key_col >= 0) & (key_col < SIDE * n_wa)
    ).astype(F32)

    def attend(key, value, part):
        cols = slice(COUNT * (1 + part), COUNT * (2 + part))
        mask = table_v[:, cols].astype(F32) * inside[:, COUNT * part : COUNT * (part + 1)]
        sums = []
        for first in range(2):
            weights, values = [], []
            for h in range(first, HEADS, 2):
                raw = dot_t(queries[h], key) * (sf_s[h] * (LOG2E / HD))
                weights.append((jnp.exp2(raw) * mask).astype(BF))
                count = jnp.where(lane_head == h + 1 - 2 * first, one, zero)
                values.append(jnp.where(lane_head == h, value, count))
            sums.append(dot(jnp.concatenate(weights, 1), jnp.concatenate(values, 0)))
        return sums

    loads["sf"].wait()
    own_a, own_b = attend(head_norm(proj[:, C : 2 * C]), proj[:, 2 * C :].astype(BF), 0)

    for copy in halos:
        copy.wait_recv()
    proj_h = dot(halo_v[...], qkv_v[:, C:])
    halo_a, halo_b = attend(head_norm(proj_h[:, :C]), proj_h[:, C:].astype(BF), 1)
    sum_a, sum_b = own_a + halo_a, own_b + halo_b
    even = lax.rem(lane_head, 2) == 0
    over = jnp.where(even, sum_a, sum_b)
    under = jnp.where(even, sum_b, sum_a)
    under = jnp.concatenate(
        [pltpu.roll(under[:, :128], HD, 1), pltpu.roll(under[:, 128:], HD, 1)], 1
    )
    attn = (over / under).astype(BF)

    loads["out"].wait()
    loads["gf"].wait()
    h1 = (tok_v[...].astype(F32) + dot(attn, out_v[...])).astype(BF)
    h1f = h1.astype(F32)
    n2 = rms(h1f, gf_v[...]).astype(BF)
    loads["fin"].wait()
    loads["fout"].wait()
    acc = h1f
    for part in range(FFH // C):
        cols = slice(part * C, (part + 1) * C)
        gate = dot(n2, fin_v[:, cols])
        lift = dot(n2, fin_v[:, FFH + part * C : FFH + (part + 1) * C])
        gated = (jax.nn.gelu(gate, approximate=True) * lift).astype(BF)
        acc = acc + dot(gated, fout_v[cols, :])
    fine = acc.astype(BF)
    pooled = jnp.mean(fine.astype(F32), 0, keepdims=True).astype(BF)

    row = pooled.astype(F32)
    row_v[...] = row
    rows = spread(row_v, rows_v, row_send, row_recv, row_peers)
    fine_o[...] = fine

    loads["up"].wait()
    loads["gc"].wait()
    loads["sc"].wait()
    loads["qkvc"].wait()
    own = jnp.broadcast_to(row, (HEADS_C, C)).astype(BF)
    coarse_own = dot(own, up_v[...]).astype(BF)
    coarse_f = coarse_own.astype(F32)
    factor = lax.rsqrt(jnp.mean(coarse_f * coarse_f, -1, keepdims=True) + EPS)
    nc_own = (coarse_f * factor * gc_v[...]).astype(BF)
    cqk = dot(nc_own, qkvc_v[:, : 2 * CC])
    head_of_row = lax.broadcasted_iota(jnp.int32, (HEADS_C, CC), 0)
    diag = head_of_row == lax.broadcasted_iota(jnp.int32, (HEADS_C, CC), 1) // HD

    def norm_of(values):
        return lax.rsqrt(jnp.sum(values * values, -1, keepdims=True) * (1 / HD) + EPS)

    ck = jnp.where(diag, cqk[:, CC:], 0.0)
    slot = lax.broadcasted_iota(jnp.int32, (HEADS_C, LANES), 0)
    lane = lax.broadcasted_iota(jnp.int32, (HEADS_C, LANES), 1)
    scales = jnp.zeros((HEADS_C, 1), F32)
    for h in range(HEADS_C):
        scales = jnp.where(slot[:, 0:1] == h, sc_s[h] * (LOG2E / HD), scales)
    norms = jnp.where(slot == lane, norm_of(ck) * factor * scales, 0.0)
    norms = jnp.sum(norms, 0, keepdims=True)
    norms = jnp.where(lane[0:1] == HEADS_C, factor[0:1], norms)
    norm_v[...] = norms
    more = spread(norm_v, norms_v, norm_send, norm_recv, row_peers)
    cq = jnp.where(diag, cqk[:, :CC], 0.0)
    cq = (cq * norm_of(cq)).astype(BF)

    def gathered(own_row, others, width):
        at = lax.broadcasted_iota(jnp.int32, (g_row, width), 0)
        tile = jnp.broadcast_to(own_row, (g_row, width))
        for d in range(1, g_row):
            tile = jnp.where(at == d, others[d], tile)
        return tile

    for copy in rows:
        copy.wait_recv()
    tile = gathered(row, rows_v, C).astype(BF)
    tile_v[...] = tile
    tiles = spread(tile_v, tiles_v, tile_send, tile_recv, tile_peers)
    tiles_v[0] = tile
    for copy in more:
        copy.wait_recv()
    tile = gathered(norms, norms_v, LANES)
    ntile_v[...] = tile
    ntiles = spread(ntile_v, ntiles_v, ntile_send, ntile_recv, tile_peers)
    ntiles_v[0] = tile

    back = dot_t(cq, qkvc_v[:, CC : 2 * CC]) * gc_v[...]
    back = dot_t(jnp.concatenate(split(back), 0), up_v[...])
    back = jnp.concatenate(split(back[:HEADS_C] + back[HEADS_C:]), 1)

    for copy in tiles:
        copy.wait_recv()
    every = tiles_v[...].reshape(g_tile * g_row, C)
    scores = dot_t(back, jnp.concatenate([every, every], 1))
    for copy in ntiles:
        copy.wait_recv()
    norms = ntiles_v[...].reshape(g_tile * g_row, LANES).T
    cexp = jnp.exp2(scores * norms[:HEADS_C])
    cweights = (cexp / jnp.sum(cexp, -1, keepdims=True)) * norms[HEADS_C : HEADS_C + 1]
    mixed = dot(jnp.concatenate(split(cweights), 0), every)
    mixed = mixed[:HEADS_C] + mixed[HEADS_C:]
    mixed = dot(jnp.concatenate(split(mixed), 0), up_v[...])
    mixed = ((mixed[:HEADS_C] + mixed[HEADS_C:]) * gc_v[...]).astype(BF)
    cattn = jnp.where(diag, dot(mixed, qkvc_v[:, 2 * CC :]), 0.0)
    cattn = jnp.sum(cattn, 0, keepdims=True)
    loads["outc"].wait()
    cattn = jnp.broadcast_to(cattn, (HEADS_C, CC)).astype(BF)
    result = coarse_f + dot(cattn, outc_v[...])
    coarse_o[...] = result[0:1].astype(BF)

    for copy in halos + rows + more + tiles + ntiles:
        copy.wait_send()


def finish(fine, coarse, fine_o, coarse_o, sem):
    copies = [
        pltpu.make_async_copy(fine, fine_o, sem.at[0]),
        pltpu.make_async_copy(coarse, coarse_o, sem.at[1]),
    ]
    for copy in copies:
        copy.start()
    for copy in copies:
        copy.wait()


def solution(mesh):
    sizes = (mesh.shape["ha"], mesh.shape["wa"])
    g_row, g_tile = sizes[1], sizes[0]
    table, place = tables()
    table, place = jnp.asarray(table, BF), jnp.asarray(place)

    def shards(
        tokens,
        gain_attn,
        qkv_fine,
        scale_fine,
        out_fine,
        gain_ffn,
        ffn_in,
        ffn_out,
        up_proj,
        gain_coarse,
        qkv_coarse,
        scale_coarse,
        out_coarse,
    ):
        hbm = pl.BlockSpec(memory_space=pl.ANY)
        fine, coarse = pl.pallas_call(
            functools.partial(kernel, sizes),
            out_shape=(pltpu.VMEM((COUNT, C), BF), pltpu.VMEM((1, CC), BF)),
            in_specs=[hbm] * 15,
            out_specs=(pl.BlockSpec(memory_space=pltpu.VMEM),) * 2,
            scratch_shapes=[
                pltpu.VMEM((COUNT, C), BF),
                pltpu.VMEM((1, C), F32),
                pltpu.VMEM((C, 3 * C), BF),
                pltpu.VMEM((C, C), BF),
                pltpu.VMEM((1, C), F32),
                pltpu.VMEM((C, 2 * FFH), BF),
                pltpu.VMEM((FFH, C), BF),
                pltpu.VMEM((C, CC), BF),
                pltpu.VMEM((1, CC), F32),
                pltpu.VMEM((CC, 3 * CC), BF),
                pltpu.VMEM((CC, CC), BF),
                pltpu.VMEM((COUNT, 4 * COUNT), BF),
                pltpu.VMEM((8, 2 * COUNT), jnp.int32),
                pltpu.SMEM((HEADS,), F32),
                pltpu.SMEM((HEADS_C,), F32),
                pltpu.VMEM((COUNT, C), BF),
                pltpu.VMEM((COUNT, C), BF),
                pltpu.VMEM((1, C), F32),
                pltpu.VMEM((g_row, 1, C), F32),
                pltpu.VMEM((1, LANES), F32),
                pltpu.VMEM((g_row, 1, LANES), F32),
                pltpu.VMEM((g_row, C), BF),
                pltpu.VMEM((g_tile, g_row, C), BF),
                pltpu.VMEM((g_row, LANES), F32),
                pltpu.VMEM((g_tile, g_row, LANES), F32),
                pltpu.SemaphoreType.DMA((15,)),
                pltpu.SemaphoreType.DMA((8,)),
                pltpu.SemaphoreType.DMA((8,)),
                pltpu.SemaphoreType.DMA((g_row,)),
                pltpu.SemaphoreType.DMA((g_row,)),
                pltpu.SemaphoreType.DMA((g_row,)),
                pltpu.SemaphoreType.DMA((g_row,)),
                pltpu.SemaphoreType.DMA((g_tile,)),
                pltpu.SemaphoreType.DMA((g_tile,)),
                pltpu.SemaphoreType.DMA((g_tile,)),
                pltpu.SemaphoreType.DMA((g_tile,)),
            ],
            compiler_params=pltpu.CompilerParams(
                collective_id=0, has_side_effects=True, vmem_limit_bytes=VMEM
            ),
        )(*[pltpu.with_memory_space_constraint(v, pltpu.HBM) for v in (
            tokens.reshape(COUNT, C),
            gain_attn.reshape(1, C),
            qkv_fine,
            scale_fine,
            out_fine,
            gain_ffn.reshape(1, C),
            ffn_in,
            ffn_out,
            up_proj,
            gain_coarse.reshape(1, CC),
            qkv_coarse,
            scale_coarse,
            out_coarse,
            table,
            place,
        )])
        fine, coarse = pl.pallas_call(
            finish,
            out_shape=(
                jax.ShapeDtypeStruct((COUNT, C), BF),
                jax.ShapeDtypeStruct((1, CC), BF),
            ),
            in_specs=[pl.BlockSpec(memory_space=pltpu.VMEM)] * 2,
            out_specs=(pl.BlockSpec(memory_space=pltpu.HBM),) * 2,
            scratch_shapes=[pltpu.SemaphoreType.DMA((2,))],
            compiler_params=pltpu.CompilerParams(vmem_limit_bytes=1024 * 1024),
        )(fine, coarse)
        return fine.reshape(SIDE, SIDE, C), coarse.reshape(1, 1, CC)

    return jax.shard_map(
        shards,
        mesh=mesh,
        in_specs=(P("ha", "wa", None),) + (P(),) * 12,
        out_specs=(P("ha", "wa", None), P("ha", "wa", None)),
        check_vma=False,
    )
```

time: 35.2 us -> 31.8 us (0.903)
  local copies, waits for them, and re-layouts: 2.85 us -> 0 us
  Pallas kernels: 31.5 us -> 31 us
    unnamed x2 -> x0, local copies, waits for them, and re-layouts: 2.85 us -> none
    pallas_call x1 -> x2, Pallas kernels: 31.5 us -> 31 us  [the longest x1 30.4 us: shards(): pl.pallas_call(functools.partial(kernel, sizes), out_shape=(pltpu.VMEM((C...]
where the time goes in v2:
time: 31.8 us; the launch traced here: 31.7 us
  Pallas kernels  31 us (97%)
  between operations  0.64 us (2%)
    pallas_call x1, Pallas kernels, shards(): pl.pallas_call(functools.partial(kernel, sizes), out_shape=(pltpu.VMEM((C...  30.4 us
    pallas_call x1, Pallas kernels, shards(): pl.pallas_call(finish, out_shape=(jax.ShapeDtypeStruct((COUNT, C), BF), j...  0.68 us

profile of v2, /device:TPU:1, one launch (start us, length us, event | category | flops | bytes accessed | tf_op | source)
XLA Modules:
  0.0 31.7 jit_solution(6997493748932494528)
XLA Ops:
  0.6 30.4 %shard_map.158 = (bf16[256,256]{1,0:T(8,128)(2,1)S(1)}, bf16[1,1024]{1,0:T(2,128)(2,1)S(1)}) custom-call(bf16[256,256]{1,0:T(8,128)(2,1)} %bitcast.6, f32[1,256]{1,0:T(1,128)} %bitcast.8, bf16[256,768]{1,0:T(8,128)(2,1)} %qkv_fine.1, f32[4]{0:T(128)} %scale_fine.1, bf16[256,256]{1,0:T(8,128)(2,1)} %out_fine.1, f32[1,256]{1,0:T(1,128)} %bitcast.9, ...), custom_call_target="tpu_custom_call" | custom-call | tf_op jit(solution)/shard_map/pallas_call | solution.py:420
  31.0 0.7 %shard_map.159 = (bf16[256,256]{1,0:T(8,128)(2,1)}, bf16[1,1024]{1,0:T(2,128)(2,1)}) custom-call(bf16[256,256]{1,0:T(8,128)(2,1)S(1)} %get-tuple-element.6.fine, bf16[1,1024]{1,0:T(2,128)(2,1)S(1)} %get-tuple-element.7.coarse), custom_call_target="tpu_custom_call" | custom-call | tf_op jit(solution)/shard_map/pallas_call | solution.py:483

commit v3 on v2

v3 whole, which is shorter than its diff:
```python
import functools

import jax
import jax.numpy as jnp
import numpy as np
from jax import lax
from jax.experimental import pallas as pl
from jax.experimental.pallas import tpu as pltpu
from jax.sharding import PartitionSpec as P

C = 256
CC = 1024
HD = 64
FFH = 768
RADIUS = 3
SIDE = 16
COUNT = SIDE * SIDE
EDGE = 160
HEADS = 4
HEADS_C = 16
LANES = 128
EPS = 1e-06
VMEM = 40 * 1024 * 1024
LOG2E = 1.4426950408889634
GELU = 0.7978845608028654
MESH = pl.DeviceIdType.MESH
BF = jnp.bfloat16
F32 = jnp.float32

PIECES = (
    (-1, 0, 0, 48),
    (1, 0, 48, 48),
    (0, -1, 96, 48),
    (0, 1, 144, 48),
    (-1, -1, 192, 16),
    (-1, 1, 208, 16),
    (1, -1, 224, 16),
    (1, 1, 240, 16),
)


def tables():
    span = {-1: range(SIDE - RADIUS, SIDE), 0: range(SIDE), 1: range(RADIUS)}
    pick = np.zeros((COUNT, COUNT))
    row = np.full((COUNT,), -100, np.int32)
    col = np.full((COUNT,), -100, np.int32)
    for side_r, side_c, first, _ in PIECES:
        at = first
        for r in span[side_r]:
            for c in span[side_c]:
                pick[at, r * SIDE + c] = 1
                row[at] = r + SIDE * side_r
                col[at] = c + SIDE * side_c
                at += 1
    natural = np.arange(COUNT)
    own_r, own_c = natural // SIDE, natural % SIDE
    inner = np.minimum(
        np.minimum(own_r, SIDE - 1 - own_r), np.minimum(own_c, SIDE - 1 - own_c)
    )
    order = np.argsort(inner, kind="stable")
    perm = np.eye(COUNT)[order]
    own_r, own_c = own_r[order][:, None], own_c[order][:, None]

    def near(key_r, key_c):
        return (np.abs(key_r - own_r) <= RADIUS) & (np.abs(key_c - own_c) <= RADIUS)

    heads = (natural[:, None] // HD) == (natural[None] // HD)
    parts = [perm, perm.T, near(natural // SIDE, natural % SIDE), near(row[None], col[None])]
    place = np.zeros((8, COUNT), np.int32)
    place[0], place[1] = row, col
    return np.concatenate([pick, heads], 1), np.concatenate(parts, 1), place


def dot(a, b):
    return jnp.dot(a, b, preferred_element_type=F32)


def dot_t(a, b):
    return lax.dot_general(a, b, (((1,), (1,)), ((), ())), preferred_element_type=F32)


def split(values):
    high = values.astype(BF)
    return high, (values - high.astype(F32)).astype(BF)


def rms(values, gain):
    return values * lax.rsqrt(jnp.mean(values * values, -1, keepdims=True) + EPS) * gain


def kernel(
    sizes,
    tokens,
    gain_attn,
    qkv_fine,
    scale_fine,
    out_fine,
    gain_ffn,
    ffn_in,
    ffn_out,
    up_proj,
    gain_coarse,
    qkv_coarse,
    scale_coarse,
    out_coarse,
    pick,
    table,
    place,
    fine_o,
    coarse_o,
    tok_v,
    ga_v,
    qkv_v,
    out_v,
    gf_v,
    fin_v,
    fout_v,
    up_v,
    gc_v,
    qkvc_v,
    outc_v,
    pick_v,
    table_v,
    place_v,
    sf_s,
    sc_s,
    send_v,
    halo_v,
    tok_p,
    own_v,
    mask_v,
    part_v,
    fine_v,
    out_m,
    row_v,
    rows_v,
    norm_v,
    norms_v,
    tile_v,
    tiles_v,
    ntile_v,
    ntiles_v,
    local_sem,
    halo_send,
    halo_recv,
    row_send,
    row_recv,
    norm_send,
    norm_recv,
    tile_send,
    tile_recv,
    ntile_send,
    ntile_recv,
):
    n_ha, n_wa = sizes
    n_x, n_z = n_ha // 4, n_wa // 2
    g_row, g_tile = n_z * 2, n_x * 4
    ha, wa = lax.axis_index("ha"), lax.axis_index("wa")
    core = lax.rem(ha, 2)
    x = lax.div(ha, 4)
    z = lax.div(wa, 2)
    y = lax.rem(lax.div(ha, 2), 2) * 2 + lax.rem(wa, 2)

    def far(step, count):
        return min(step, count - step)

    neighbours = []
    for side_r, side_c, _, _ in PIECES:
        neighbours.append((lax.rem(ha - side_r + n_ha, n_ha), lax.rem(wa - side_c + n_wa, n_wa)))
    row_peers = []
    for d in sorted(range(1, g_row), key=lambda d: -far(d // 2, n_z)):
        to_z = lax.rem(z + d // 2, n_z)
        to_core = lax.rem(core + d % 2, 2)
        row_peers.append((d, (ha - core + to_core, wa - 2 * z + 2 * to_z)))
    tile_peers = []
    for d in sorted(range(1, g_tile), key=lambda d: -far(d // 4, n_x) - far(d % 4, 4)):
        to_x = lax.rem(x + d // 4, n_x)
        to_y = lax.rem(y + d % 4, 4)
        peer = (4 * to_x + 2 * lax.div(to_y, 2) + core, 2 * z + lax.rem(to_y, 2))
        tile_peers.append((d, peer))
    names = ("tok", "ga", "qkv", "pick", "table", "place", "sf", "out", "gf", "fin", "fout")
    names += ("up", "gc", "sc", "qkvc", "outc")
    pairs = {
        "tok": (tokens, tok_v),
        "ga": (gain_attn, ga_v),
        "pick": (pick, pick_v),
        "table": (table, table_v),
        "place": (place, place_v),
        "qkv": (qkv_fine, qkv_v),
        "sf": (scale_fine, sf_s),
        "out": (out_fine, out_v),
        "gf": (gain_ffn, gf_v),
        "fin": (ffn_in, fin_v),
        "fout": (ffn_out, fout_v),
        "up": (up_proj, up_v),
        "gc": (gain_coarse, gc_v),
        "sc": (scale_coarse, sc_s),
        "qkvc": (qkv_coarse, qkvc_v),
        "outc": (out_coarse, outc_v),
    }
    loads = {}
    for i, name in enumerate(names):
        loads[name] = pltpu.make_async_copy(*pairs[name], local_sem.at[i])
    for name in names[:4]:
        loads[name].start()
    barrier = pltpu.get_barrier_semaphore()
    hops = [(far(d // 2, n_z), peer) for d, peer in row_peers]
    hops += [(far(d // 4, n_x) + far(d % 4, 4), peer) for d, peer in tile_peers]
    hops += [(3 if PIECES[i][0] else 2, peer) for i, peer in enumerate(neighbours)]
    for _, peer in sorted(hops, key=lambda hop: -hop[0]):
        pl.semaphore_signal(barrier, inc=1, device_id=peer, device_id_type=MESH)

    for name in names[4:]:
        loads[name].start()

    def spread(src, dst, send_sem, recv_sem, peers):
        for d, peer in peers:
            pltpu.make_async_remote_copy(
                src_ref=src,
                dst_ref=dst.at[d],
                send_sem=send_sem,
                recv_sem=recv_sem,
                device_id=peer,
                device_id_type=MESH,
            ).start()
        others = dst.at[pl.ds(1, len(peers))]
        return pltpu.make_async_remote_copy(
            src_ref=others,
            dst_ref=others,
            send_sem=send_sem,
            recv_sem=recv_sem,
            device_id=peers[0][1],
            device_id_type=MESH,
        )

    loads["tok"].wait()
    loads["ga"].wait()
    normed = rms(tok_v[...].astype(F32), ga_v[...]).astype(BF)
    loads["qkv"].wait()
    proj = dot(normed, qkv_v[...])
    loads["pick"].wait()
    same = pick_v[:, COUNT:]

    def head_norm(values):
        high, low = split(values * values)
        size = (dot(high, same) + dot(low, same)) * (1 / HD)
        return values * lax.rsqrt(size + EPS)

    key, value = head_norm(proj[:, C : 2 * C]).astype(BF), proj[:, 2 * C :].astype(BF)
    send_v[...] = dot(pick_v[:, :COUNT], jnp.concatenate([key, value], 1)).astype(BF)

    pl.semaphore_wait(barrier, len(neighbours) + len(row_peers) + len(tile_peers))
    for i, (_, _, first, rows) in enumerate(PIECES):
        pltpu.make_async_remote_copy(
            src_ref=send_v.at[pl.ds(first, rows)],
            dst_ref=halo_v.at[pl.ds(first, rows)],
            send_sem=halo_send,
            recv_sem=halo_recv,
            device_id=neighbours[i],
            device_id_type=MESH,
        ).start()
    halos = pltpu.make_async_remote_copy(
        src_ref=send_v,
        dst_ref=halo_v,
        send_sem=halo_send,
        recv_sem=halo_recv,
        device_id=neighbours[0],
        device_id_type=MESH,
    )

    loads["table"].wait()
    loads["place"].wait()
    loads["sf"].wait()
    perm = table_v[:, :COUNT]
    tok_p[...] = dot(perm, tok_v[...]).astype(BF)
    lane_head = lax.broadcasted_iota(jnp.int32, (COUNT, C), 1) // HD
    scales = jnp.zeros((1, C), F32)
    for h in range(HEADS):
        scales = jnp.where(lane_head[0:1] == h, sf_s[h] * (LOG2E / HD), scales)
    query = dot(perm, (head_norm(proj[:, :C]) * scales).astype(BF)).astype(BF)
    zero, one = jnp.zeros((COUNT, C), BF), jnp.ones((COUNT, C), BF)
    queries = [jnp.where(lane_head == h, query, zero) for h in range(HEADS)]

    key_row = place_v[0:1, :] + ha * SIDE
    key_col = place_v[1:2, :] + wa * SIDE
    inside = (
        (key_row >= 0) & (key_row < SIDE * n_ha) & (key_col >= 0) & (key_col < SIDE * n_wa)
    ).astype(F32)
    mask_v[...] = table_v[:EDGE, 3 * COUNT : 4 * COUNT].astype(F32) * inside

    def attend(rows, keys, value, mask):
        sums = []
        for first in range(2):
            weights, values = [], []
            for h in range(first, HEADS, 2):
                raw = dot_t(queries[h][:rows], keys)
                weights.append((jnp.exp2(raw) * mask).astype(BF))
                count = jnp.where(lane_head == h + 1 - 2 * first, one, zero)
                values.append(jnp.where(lane_head == h, value, count))
            sums.append(dot(jnp.concatenate(weights, 1), jnp.concatenate(values, 0)))
        return sums

    def finished(sum_a, sum_b, tok):
        even = lax.rem(lane_head[: tok.shape[0]], 2) == 0
        over = jnp.where(even, sum_a, sum_b)
        under = jnp.where(even, sum_b, sum_a)
        under = jnp.concatenate(
            [pltpu.roll(under[:, :LANES], HD, 1), pltpu.roll(under[:, LANES:], HD, 1)], 1
        )
        attn = (over / under).astype(BF)
        h1 = (tok.astype(F32) + dot(attn, out_v[...])).astype(BF)
        h1 = h1.astype(F32)
        n2 = rms(h1, gf_v[...]).astype(BF)
        acc = 0.0
        for part in range(FFH // C):
            gate = dot(n2, fin_v[:, part * C : (part + 1) * C])
            lift = dot(n2, fin_v[:, FFH + part * C : FFH + (part + 1) * C])
            bend = jnp.tanh(gate * (GELU + (GELU * 0.044715) * (gate * gate)))
            gated = (gate * lift * (1.0 + bend)).astype(BF)
            acc = acc + dot(gated, fout_v[part * C : (part + 1) * C, :])
        return (h1 + 0.5 * acc).astype(BF)

    own_mask = table_v[:, 2 * COUNT : 3 * COUNT].astype(F32)
    sum_a, sum_b = attend(COUNT, key, value, own_mask)
    own_v[0] = sum_a[:EDGE]
    own_v[1] = sum_b[:EDGE]
    for name in ("out", "gf", "fin", "fout"):
        loads[name].wait()
    fine = finished(sum_a[EDGE:], sum_b[EDGE:], tok_p[EDGE:, :])
    fine_v[EDGE:, :] = fine
    part_v[...] = jnp.sum(fine.astype(F32), 0, keepdims=True)

    halos.wait_recv()
    sum_a, sum_b = attend(EDGE, halo_v[:, :C], halo_v[:, C:], mask_v[...])
    fine = finished(own_v[0] + sum_a, own_v[1] + sum_b, tok_p[:EDGE, :])
    fine_v[:EDGE, :] = fine
    pooled = part_v[...] + jnp.sum(fine.astype(F32), 0, keepdims=True)
    pooled = (pooled * (1 / COUNT)).astype(BF)

    row = pooled.astype(F32)
    row_v[...] = row
    rows = spread(row_v, rows_v, row_send, row_recv, row_peers)
    fine_o[...] = dot(table_v[:, COUNT : 2 * COUNT], fine_v[...]).astype(BF)

    loads["up"].wait()
    loads["gc"].wait()
    loads["sc"].wait()
    loads["qkvc"].wait()
    own = jnp.broadcast_to(row, (HEADS_C, C)).astype(BF)
    coarse_own = dot(own, up_v[...]).astype(BF)
    coarse_f = coarse_own.astype(F32)
    factor = lax.rsqrt(jnp.mean(coarse_f * coarse_f, -1, keepdims=True) + EPS)
    nc_own = (coarse_f * factor * gc_v[...]).astype(BF)
    cqk = dot(nc_own, qkvc_v[:, : 2 * CC])
    head_of_row = lax.broadcasted_iota(jnp.int32, (HEADS_C, CC), 0)
    diag = head_of_row == lax.broadcasted_iota(jnp.int32, (HEADS_C, CC), 1) // HD

    def norm_of(values):
        return lax.rsqrt(jnp.sum(values * values, -1, keepdims=True) * (1 / HD) + EPS)

    ck = jnp.where(diag, cqk[:, CC:], 0.0)
    slot = lax.broadcasted_iota(jnp.int32, (HEADS_C, LANES), 0)
    lane = lax.broadcasted_iota(jnp.int32, (HEADS_C, LANES), 1)
    scales = jnp.zeros((HEADS_C, 1), F32)
    for h in range(HEADS_C):
        scales = jnp.where(slot[:, 0:1] == h, sc_s[h] * (LOG2E / HD), scales)
    norms = jnp.where(slot == lane, norm_of(ck) * factor * scales, 0.0)
    norms = jnp.sum(norms, 0, keepdims=True)
    norms = jnp.where(lane[0:1] == HEADS_C, factor[0:1], norms)
    norm_v[...] = norms
    more = spread(norm_v, norms_v, norm_send, norm_recv, row_peers)
    cq = jnp.where(diag, cqk[:, :CC], 0.0)
    cq = (cq * norm_of(cq)).astype(BF)

    back = dot_t(cq, qkvc_v[:, CC : 2 * CC]) * gc_v[...]
    back = dot_t(jnp.concatenate(split(back), 0), up_v[...])
    back = jnp.concatenate(split(back[:HEADS_C] + back[HEADS_C:]), 1)

    def gathered(own_row, others, width):
        at = lax.broadcasted_iota(jnp.int32, (g_row, width), 0)
        tile = jnp.broadcast_to(own_row, (g_row, width))
        for d in range(1, g_row):
            tile = jnp.where(at == d, others[d], tile)
        return tile

    rows.wait_recv()
    tile = gathered(row, rows_v, C).astype(BF)
    tile_v[...] = tile
    tiles = spread(tile_v, tiles_v, tile_send, tile_recv, tile_peers)
    tiles_v[0] = tile
    more.wait_recv()
    tile = gathered(norms, norms_v, LANES)
    ntile_v[...] = tile
    ntiles = spread(ntile_v, ntiles_v, ntile_send, ntile_recv, tile_peers)
    ntiles_v[0] = tile

    high, low = split(up_v[...].astype(F32) * gc_v[...])
    value = qkvc_v[:, 2 * CC :]
    out_m[...] = (dot(high, value) + dot(low, value)).astype(BF)

    tiles.wait_recv()
    every = tiles_v[...].reshape(g_tile * g_row, C)
    scores = dot_t(back, jnp.concatenate([every, every], 1))
    ntiles.wait_recv()
    norms = ntiles_v[...].reshape(g_tile * g_row, LANES).T
    cexp = jnp.exp2(scores * norms[:HEADS_C])
    cweights = (cexp / jnp.sum(cexp, -1, keepdims=True)) * norms[HEADS_C : HEADS_C + 1]
    mixed = dot(jnp.concatenate(split(cweights), 0), every)
    mixed = mixed[:HEADS_C] + mixed[HEADS_C:]
    mixed = dot(jnp.concatenate(split(mixed), 0), out_m[...])
    cattn = jnp.where(diag, mixed[:HEADS_C] + mixed[HEADS_C:], 0.0)
    cattn = jnp.sum(cattn, 0, keepdims=True)
    loads["outc"].wait()
    cattn = jnp.broadcast_to(cattn, (HEADS_C, CC)).astype(BF)
    result = coarse_f + dot(cattn, outc_v[...])
    coarse_o[...] = result[0:1].astype(BF)

    for copy in (halos, rows, more, tiles, ntiles):
        copy.wait_send()


def finish(fine, coarse, fine_o, coarse_o, sem):
    copies = [
        pltpu.make_async_copy(fine, fine_o, sem.at[0]),
        pltpu.make_async_copy(coarse, coarse_o, sem.at[1]),
    ]
    for copy in copies:
        copy.start()
    for copy in copies:
        copy.wait()


def solution(mesh):
    sizes = (mesh.shape["ha"], mesh.shape["wa"])
    g_row, g_tile = sizes[1], sizes[0]
    pick, table, place = tables()
    pick, table = jnp.asarray(pick, BF), jnp.asarray(table, BF)
    place = jnp.asarray(place)

    def shards(
        tokens,
        gain_attn,
        qkv_fine,
        scale_fine,
        out_fine,
        gain_ffn,
        ffn_in,
        ffn_out,
        up_proj,
        gain_coarse,
        qkv_coarse,
        scale_coarse,
        out_coarse,
    ):
        hbm = pl.BlockSpec(memory_space=pl.ANY)
        fine, coarse = pl.pallas_call(
            functools.partial(kernel, sizes),
            out_shape=(pltpu.VMEM((COUNT, C), BF), pltpu.VMEM((1, CC), BF)),
            in_specs=[hbm] * 16,
            out_specs=(pl.BlockSpec(memory_space=pltpu.VMEM),) * 2,
            scratch_shapes=[
                pltpu.VMEM((COUNT, C), BF),
                pltpu.VMEM((1, C), F32),
                pltpu.VMEM((C, 3 * C), BF),
                pltpu.VMEM((C, C), BF),
                pltpu.VMEM((1, C), F32),
                pltpu.VMEM((C, 2 * FFH), BF),
                pltpu.VMEM((FFH, C), BF),
                pltpu.VMEM((C, CC), BF),
                pltpu.VMEM((1, CC), F32),
                pltpu.VMEM((CC, 3 * CC), BF),
                pltpu.VMEM((CC, CC), BF),
                pltpu.VMEM((COUNT, 2 * COUNT), BF),
                pltpu.VMEM((COUNT, 4 * COUNT), BF),
                pltpu.VMEM((8, COUNT), jnp.int32),
                pltpu.SMEM((HEADS,), F32),
                pltpu.SMEM((HEADS_C,), F32),
                pltpu.VMEM((COUNT, 2 * C), BF),
                pltpu.VMEM((COUNT, 2 * C), BF),
                pltpu.VMEM((COUNT, C), BF),
                pltpu.VMEM((2, EDGE, C), F32),
                pltpu.VMEM((EDGE, COUNT), F32),
                pltpu.VMEM((1, C), F32),
                pltpu.VMEM((COUNT, C), BF),
                pltpu.VMEM((C, CC), BF),
                pltpu.VMEM((1, C), F32),
                pltpu.VMEM((g_row, 1, C), F32),
                pltpu.VMEM((1, LANES), F32),
                pltpu.VMEM((g_row, 1, LANES), F32),
                pltpu.VMEM((g_row, C), BF),
                pltpu.VMEM((g_tile, g_row, C), BF),
                pltpu.VMEM((g_row, LANES), F32),
                pltpu.VMEM((g_tile, g_row, LANES), F32),
                pltpu.SemaphoreType.DMA((16,)),
                *[pltpu.SemaphoreType.DMA] * 10,
            ],
            compiler_params=pltpu.CompilerParams(
                collective_id=0, has_side_effects=True, vmem_limit_bytes=VMEM
            ),
        )(*[pltpu.with_memory_space_constraint(v, pltpu.HBM) for v in (
            tokens.reshape(COUNT, C),
            gain_attn.reshape(1, C),
            qkv_fine,
            scale_fine,
            out_fine,
            gain_ffn.reshape(1, C),
            ffn_in,
            ffn_out,
            up_proj,
            gain_coarse.reshape(1, CC),
            qkv_coarse,
            scale_coarse,
            out_coarse,
            pick,
            table,
            place,
        )])
        fine, coarse = pl.pallas_call(
            finish,
            out_shape=(
                jax.ShapeDtypeStruct((COUNT, C), BF),
                jax.ShapeDtypeStruct((1, CC), BF),
            ),
            in_specs=[pl.BlockSpec(memory_space=pltpu.VMEM)] * 2,
            out_specs=(pl.BlockSpec(memory_space=pltpu.HBM),) * 2,
            scratch_shapes=[pltpu.SemaphoreType.DMA((2,))],
            compiler_params=pltpu.CompilerParams(vmem_limit_bytes=1024 * 1024),
        )(fine, coarse)
        return fine.reshape(SIDE, SIDE, C), coarse.reshape(1, 1, CC)

    return jax.shard_map(
        shards,
        mesh=mesh,
        in_specs=(P("ha", "wa", None),) + (P(),) * 12,
        out_specs=(P("ha", "wa", None), P("ha", "wa", None)),
        check_vma=False,
    )
```

time: 31.8 us -> 29.3 us (0.921)
  Pallas kernels: 31 us -> 28.6 us
    pallas_call x1, Pallas kernels: 30.4 us -> 27.9 us  [shards(): pl.pallas_call(functools.partial(kernel, sizes), out_shape=(pltpu.VMEM((C...]
where the time goes in v3:
time: 29.3 us; the launch traced here: 29.2 us
  Pallas kernels  28.6 us (98%)
  between operations  0.64 us (2%)
    pallas_call x1, Pallas kernels, shards(): pl.pallas_call(functools.partial(kernel, sizes), out_shape=(pltpu.VMEM((C...  27.9 us
    pallas_call x1, Pallas kernels, shards(): pl.pallas_call(finish, out_shape=(jax.ShapeDtypeStruct((COUNT, C), BF), j...  0.68 us

profile of v3, /device:TPU:1, one launch (start us, length us, event | category | flops | bytes accessed | tf_op | source)
XLA Modules:
  0.0 29.2 jit_solution(15990859805451643616)
XLA Ops:
  0.6 27.9 %shard_map.167 = (bf16[256,256]{1,0:T(8,128)(2,1)S(1)}, bf16[1,1024]{1,0:T(2,128)(2,1)S(1)}) custom-call(bf16[256,256]{1,0:T(8,128)(2,1)} %bitcast.6, f32[1,256]{1,0:T(1,128)} %bitcast.8, bf16[256,768]{1,0:T(8,128)(2,1)} %qkv_fine.1, f32[4]{0:T(128)} %scale_fine.1, bf16[256,256]{1,0:T(8,128)(2,1)} %out_fine.1, f32[1,256]{1,0:T(1,128)} %bitcast.9, ...), custom_call_target="tpu_custom_call" | custom-call | tf_op jit(solution)/shard_map/pallas_call | solution.py:456
  28.6 0.7 %shard_map.168 = (bf16[256,256]{1,0:T(8,128)(2,1)}, bf16[1,1024]{1,0:T(2,128)(2,1)}) custom-call(bf16[256,256]{1,0:T(8,128)(2,1)S(1)} %get-tuple-element.6.fine, bf16[1,1024]{1,0:T(2,128)(2,1)S(1)} %get-tuple-element.7.coarse), custom_call_target="tpu_custom_call" | custom-call | tf_op jit(solution)/shard_map/pallas_call | solution.py:518

commit v4 on v3

--- a/solution.py
+++ b/solution.py
@@ -131,53 +131,23 @@
     mask_v,
     part_v,
     fine_v,
-    out_m,
+    key_m,
+    value_m,
     row_v,
     rows_v,
-    norm_v,
-    norms_v,
     tile_v,
     tiles_v,
-    ntile_v,
-    ntiles_v,
     local_sem,
     halo_send,
     halo_recv,
     row_send,
     row_recv,
-    norm_send,
-    norm_recv,
     tile_send,
     tile_recv,
-    ntile_send,
-    ntile_recv,
 ):
     n_ha, n_wa = sizes
     n_x, n_z = n_ha // 4, n_wa // 2
     g_row, g_tile = n_z * 2, n_x * 4
-    ha, wa = lax.axis_index("ha"), lax.axis_index("wa")
-    core = lax.rem(ha, 2)
-    x = lax.div(ha, 4)
-    z = lax.div(wa, 2)
-    y = lax.rem(lax.div(ha, 2), 2) * 2 + lax.rem(wa, 2)
-
-    def far(step, count):
-        return min(step, count - step)
-
-    neighbours = []
-    for side_r, side_c, _, _ in PIECES:
-        neighbours.append((lax.rem(ha - side_r + n_ha, n_ha), lax.rem(wa - side_c + n_wa, n_wa)))
-    row_peers = []
-    for d in sorted(range(1, g_row), key=lambda d: -far(d // 2, n_z)):
-        to_z = lax.rem(z + d // 2, n_z)
-        to_core = lax.rem(core + d % 2, 2)
-        row_peers.append((d, (ha - core + to_core, wa - 2 * z + 2 * to_z)))
-    tile_peers = []
-    for d in sorted(range(1, g_tile), key=lambda d: -far(d // 4, n_x) - far(d % 4, 4)):
-        to_x = lax.rem(x + d // 4, n_x)
-        to_y = lax.rem(y + d % 4, 4)
-        peer = (4 * to_x + 2 * lax.div(to_y, 2) + core, 2 * z + lax.rem(to_y, 2))
-        tile_peers.append((d, peer))
     names = ("tok", "ga", "qkv", "pick", "table", "place", "sf", "out", "gf", "fin", "fout")
     names += ("up", "gc", "sc", "qkvc", "outc")
     pairs = {
@@ -203,13 +173,41 @@
         loads[name] = pltpu.make_async_copy(*pairs[name], local_sem.at[i])
     for name in names[:4]:
         loads[name].start()
+    ha, wa = lax.axis_index("ha"), lax.axis_index("wa")
+    core = lax.rem(ha, 2)
+    x = lax.div(ha, 4)
+    z = lax.div(wa, 2)
+    y = lax.rem(lax.div(ha, 2), 2) * 2 + lax.rem(wa, 2)
+
+    def far(step, count):
+        return min(step, count - step)
+
+    def neighbour(i):
+        side_r, side_c = PIECES[i][:2]
+        return (lax.rem(ha - side_r + n_ha, n_ha), lax.rem(wa - side_c + n_wa, n_wa))
+
+    def row_peer(d):
+        to_z = lax.rem(z + d // 2, n_z)
+        to_core = lax.rem(core + d % 2, 2)
+        return (ha - core + to_core, wa - 2 * z + 2 * to_z)
+
+    def tile_peer(d):
+        to_x = lax.rem(x + d // 4, n_x)
+        to_y = lax.rem(y + d % 4, 4)
+        return (4 * to_x + 2 * lax.div(to_y, 2) + core, 2 * z + lax.rem(to_y, 2))
+
+    hops = [(far(d // 2, n_z), row_peer, d) for d in range(1, g_row)]
+    hops += [(far(d // 4, n_x) + far(d % 4, 4), tile_peer, d) for d in range(1, g_tile)]
+    hops += [(3 if PIECES[i][0] else 2, neighbour, i) for i in range(len(PIECES))]
+    hops.sort(key=lambda hop: -hop[0])
     barrier = pltpu.get_barrier_semaphore()
-    hops = [(far(d // 2, n_z), peer) for d, peer in row_peers]
-    hops += [(far(d // 4, n_x) + far(d % 4, 4), peer) for d, peer in tile_peers]
-    hops += [(3 if PIECES[i][0] else 2, peer) for i, peer in enumerate(neighbours)]
-    for _, peer in sorted(hops, key=lambda hop: -hop[0]):
-        pl.semaphore_signal(barrier, inc=1, device_id=peer, device_id_type=MESH)
-
+    where = {}
+    for _, of, d in hops:
+        where[of, d] = of(d)
+        pl.semaphore_signal(barrier, inc=1, device_id=where[of, d], device_id_type=MESH)
+    neighbours = [where[neighbour, i] for i in range(len(PIECES))]
+    row_peers = [(d, where[of, d]) for _, of, d in hops if of is row_peer]
+    tile_peers = [(d, where[of, d]) for _, of, d in hops if of is tile_peer]
     for name in names[4:]:
         loads[name].start()
 
@@ -249,7 +247,7 @@
     key, value = head_norm(proj[:, C : 2 * C]).astype(BF), proj[:, 2 * C :].astype(BF)
     send_v[...] = dot(pick_v[:, :COUNT], jnp.concatenate([key, value], 1)).astype(BF)
 
-    pl.semaphore_wait(barrier, len(neighbours) + len(row_peers) + len(tile_peers))
+    pl.semaphore_wait(barrier, len(hops))
     for i, (_, _, first, rows) in enumerate(PIECES):
         pltpu.make_async_remote_copy(
             src_ref=send_v.at[pl.ds(first, rows)],
@@ -330,6 +328,16 @@
     fine_v[EDGE:, :] = fine
     part_v[...] = jnp.sum(fine.astype(F32), 0, keepdims=True)
 
+    for name in ("up", "gc", "qkvc"):
+        loads[name].wait()
+    up_high, up_low = split(up_v[...].astype(F32) * gc_v[...])
+
+    def through(part):
+        after = qkvc_v[:, part * CC : (part + 1) * CC]
+        return (dot(up_high, after) + dot(up_low, after)).astype(BF)
+
+    key_m[...] = through(1)
+
     halos.wait_recv()
     sum_a, sum_b = attend(EDGE, halo_v[:, :C], halo_v[:, C:], mask_v[...])
     fine = finished(own_v[0] + sum_a, own_v[1] + sum_b, tok_p[:EDGE, :])
@@ -338,76 +346,65 @@
     pooled = (pooled * (1 / COUNT)).astype(BF)
 
     row = pooled.astype(F32)
-    row_v[...] = row
-    rows = spread(row_v, rows_v, row_send, row_recv, row_peers)
-    fine_o[...] = dot(table_v[:, COUNT : 2 * COUNT], fine_v[...]).astype(BF)
-
-    loads["up"].wait()
-    loads["gc"].wait()
     loads["sc"].wait()
-    loads["qkvc"].wait()
     own = jnp.broadcast_to(row, (HEADS_C, C)).astype(BF)
     coarse_own = dot(own, up_v[...]).astype(BF)
     coarse_f = coarse_own.astype(F32)
     factor = lax.rsqrt(jnp.mean(coarse_f * coarse_f, -1, keepdims=True) + EPS)
-    nc_own = (coarse_f * factor * gc_v[...]).astype(BF)
-    cqk = dot(nc_own, qkvc_v[:, : 2 * CC])
     head_of_row = lax.broadcasted_iota(jnp.int32, (HEADS_C, CC), 0)
     diag = head_of_row == lax.broadcasted_iota(jnp.int32, (HEADS_C, CC), 1) // HD
 
     def norm_of(values):
         return lax.rsqrt(jnp.sum(values * values, -1, keepdims=True) * (1 / HD) + EPS)
 
-    ck = jnp.where(diag, cqk[:, CC:], 0.0)
+    ck = jnp.where(diag, dot(own, key_m[...]), 0.0) * factor
     slot = lax.broadcasted_iota(jnp.int32, (HEADS_C, LANES), 0)
     lane = lax.broadcasted_iota(jnp.int32, (HEADS_C, LANES), 1)
     scales = jnp.zeros((HEADS_C, 1), F32)
     for h in range(HEADS_C):
         scales = jnp.where(slot[:, 0:1] == h, sc_s[h] * (LOG2E / HD), scales)
-    norms = jnp.where(slot == lane, norm_of(ck) * factor * scales, 0.0)
-    norms = jnp.sum(norms, 0, keepdims=True)
-    norms = jnp.where(lane[0:1] == HEADS_C, factor[0:1], norms)
-    norm_v[...] = norms
-    more = spread(norm_v, norms_v, norm_send, norm_recv, row_peers)
-    cq = jnp.where(diag, cqk[:, :CC], 0.0)
+    norms = norm_of(ck) * factor * scales
+    twice = lax.rem(lane, LANES // 2)
+    norms = jnp.sum(jnp.where(slot == twice, norms, 0.0), 0, keepdims=True)
+    norms = jnp.where(twice[0:1] == HEADS_C, factor[0:1], norms)
+    high, low = split(norms)
+    norms = jnp.where(lane[0:1] < LANES // 2, high.astype(F32), low.astype(F32))
+    row = jnp.concatenate([row, norms], 1)
+
+    row_v[...] = row
+    rows = spread(row_v, rows_v, row_send, row_recv, row_peers)
+    fine_o[...] = dot(table_v[:, COUNT : 2 * COUNT], fine_v[...]).astype(BF)
+
+    nc_own = (coarse_f * factor * gc_v[...]).astype(BF)
+    cq = jnp.where(diag, dot(nc_own, qkvc_v[:, :CC]), 0.0)
     cq = (cq * norm_of(cq)).astype(BF)
 
-    back = dot_t(cq, qkvc_v[:, CC : 2 * CC]) * gc_v[...]
-    back = dot_t(jnp.concatenate(split(back), 0), up_v[...])
-    back = jnp.concatenate(split(back[:HEADS_C] + back[HEADS_C:]), 1)
-
-    def gathered(own_row, others, width):
-        at = lax.broadcasted_iota(jnp.int32, (g_row, width), 0)
-        tile = jnp.broadcast_to(own_row, (g_row, width))
-        for d in range(1, g_row):
-            tile = jnp.where(at == d, others[d], tile)
-        return tile
+    back = jnp.concatenate(split(dot_t(cq, key_m[...])), 1)
 
     rows.wait_recv()
-    tile = gathered(row, rows_v, C).astype(BF)
+    at = lax.broadcasted_iota(jnp.int32, (g_row, C + LANES), 0)
+    tile = jnp.broadcast_to(row, (g_row, C + LANES))
+    for d in range(1, g_row):
+        tile = jnp.where(at == d, rows_v[d], tile)
+    tile = tile.astype(BF)
     tile_v[...] = tile
     tiles = spread(tile_v, tiles_v, tile_send, tile_recv, tile_peers)
     tiles_v[0] = tile
-    more.wait_recv()
-    tile = gathered(norms, norms_v, LANES)
-    ntile_v[...] = tile
-    ntiles = spread(ntile_v, ntiles_v, ntile_send, ntile_recv, tile_peers)
-    ntiles_v[0] = tile
-
-    high, low = split(up_v[...].astype(F32) * gc_v[...])
-    value = qkvc_v[:, 2 * CC :]
-    out_m[...] = (dot(high, value) + dot(low, value)).astype(BF)
+
+    value_m[...] = through(2)
 
     tiles.wait_recv()
-    every = tiles_v[...].reshape(g_tile * g_row, C)
+    every = tiles_v[...].reshape(g_tile * g_row, C + LANES)
+    norms = every[:, C:].astype(F32).T
+    norms = norms[: LANES // 2] + norms[LANES // 2 :]
+    every = every[:, :C]
     scores = dot_t(back, jnp.concatenate([every, every], 1))
-    ntiles.wait_recv()
-    norms = ntiles_v[...].reshape(g_tile * g_row, LANES).T
     cexp = jnp.exp2(scores * norms[:HEADS_C])
-    cweights = (cexp / jnp.sum(cexp, -1, keepdims=True)) * norms[HEADS_C : HEADS_C + 1]
-    mixed = dot(jnp.concatenate(split(cweights), 0), every)
-    mixed = mixed[:HEADS_C] + mixed[HEADS_C:]
-    mixed = dot(jnp.concatenate(split(mixed), 0), out_m[...])
+    rest = 1 / jnp.sum(cexp, -1, keepdims=True)
+    cexp = cexp * norms[HEADS_C : HEADS_C + 1]
+    mixed = dot(jnp.concatenate(split(cexp), 0), every)
+    mixed = (mixed[:HEADS_C] + mixed[HEADS_C:]) * rest
+    mixed = dot(jnp.concatenate(split(mixed), 0), value_m[...])
     cattn = jnp.where(diag, mixed[:HEADS_C] + mixed[HEADS_C:], 0.0)
     cattn = jnp.sum(cattn, 0, keepdims=True)
     loads["outc"].wait()
@@ -415,7 +412,7 @@
     result = coarse_f + dot(cattn, outc_v[...])
     coarse_o[...] = result[0:1].astype(BF)
 
-    for copy in (halos, rows, more, tiles, ntiles):
+    for copy in (halos, rows, tiles):
         copy.wait_send()
 
 
@@ -483,16 +480,13 @@
                 pltpu.VMEM((1, C), F32),
                 pltpu.VMEM((COUNT, C), BF),
                 pltpu.VMEM((C, CC), BF),
-                pltpu.VMEM((1, C), F32),
-                pltpu.VMEM((g_row, 1, C), F32),
-                pltpu.VMEM((1, LANES), F32),
-                pltpu.VMEM((g_row, 1, LANES), F32),
-                pltpu.VMEM((g_row, C), BF),
-                pltpu.VMEM((g_tile, g_row, C), BF),
-                pltpu.VMEM((g_row, LANES), F32),
-                pltpu.VMEM((g_tile, g_row, LANES), F32),
+                pltpu.VMEM((C, CC), BF),
+                pltpu.VMEM((1, C + LANES), F32),
+                pltpu.VMEM((g_row, 1, C + LANES), F32),
+                pltpu.VMEM((g_row, C + LANES), BF),
+                pltpu.VMEM((g_tile, g_row, C + LANES), BF),
                 pltpu.SemaphoreType.DMA((16,)),
-                *[pltpu.SemaphoreType.DMA] * 10,
+                *[pltpu.SemaphoreType.DMA] * 6,
             ],
             compiler_params=pltpu.CompilerParams(
                 collective_id=0, has_side_effects=True, vmem_limit_bytes=VMEM

time: 29.3 us -> 28.8 us (0.983)
  Pallas kernels: 28.6 us -> 28.1 us
    pallas_call x1, Pallas kernels: 27.9 us -> 27.4 us  [shards(): pl.pallas_call(functools.partial(kernel, sizes), out_shape=(pltpu.VMEM((C...]
where the time goes in v4:
time: 28.8 us
  Pallas kernels  28.1 us (98%)
  between operations  0.64 us (2%)
    pallas_call x1, Pallas kernels, shards(): pl.pallas_call(functools.partial(kernel, sizes), out_shape=(pltpu.VMEM((C...  27.4 us
    pallas_call x1, Pallas kernels, shards(): pl.pallas_call(finish, out_shape=(jax.ShapeDtypeStruct((COUNT, C), BF), j...  0.68 us

profile of v4, /device:TPU:1, one launch (start us, length us, event | category | flops | bytes accessed | tf_op | source)
XLA Modules:
  0.0 28.8 jit_solution(14090347507352360879)
XLA Ops:
  0.6 27.4 %shard_map.167 = (bf16[256,256]{1,0:T(8,128)(2,1)S(1)}, bf16[1,1024]{1,0:T(2,128)(2,1)S(1)}) custom-call(bf16[256,256]{1,0:T(8,128)(2,1)} %bitcast.6, f32[1,256]{1,0:T(1,128)} %bitcast.8, bf16[256,768]{1,0:T(8,128)(2,1)} %qkv_fine.1, f32[4]{0:T(128)} %scale_fine.1, bf16[256,256]{1,0:T(8,128)(2,1)} %out_fine.1, f32[1,256]{1,0:T(1,128)} %bitcast.9, ...), custom_call_target="tpu_custom_call" | custom-call | tf_op jit(solution)/shard_map/pallas_call | solution.py:453
  28.1 0.7 %shard_map.168 = (bf16[256,256]{1,0:T(8,128)(2,1)}, bf16[1,1024]{1,0:T(2,128)(2,1)}) custom-call(bf16[256,256]{1,0:T(8,128)(2,1)S(1)} %get-tuple-element.6.fine, bf16[1,1024]{1,0:T(2,128)(2,1)S(1)} %get-tuple-element.7.coarse), custom_call_target="tpu_custom_call" | custom-call | tf_op jit(solution)/shard_map/pallas_call | solution.py:512

commit v5 on v4

--- a/solution.py
+++ b/solution.py
@@ -287,15 +287,12 @@
     mask_v[...] = table_v[:EDGE, 3 * COUNT : 4 * COUNT].astype(F32) * inside
 
     def attend(rows, keys, value, mask):
-        sums = []
-        for first in range(2):
-            weights, values = [], []
-            for h in range(first, HEADS, 2):
-                raw = dot_t(queries[h][:rows], keys)
-                weights.append((jnp.exp2(raw) * mask).astype(BF))
-                count = jnp.where(lane_head == h + 1 - 2 * first, one, zero)
-                values.append(jnp.where(lane_head == h, value, count))
-            sums.append(dot(jnp.concatenate(weights, 1), jnp.concatenate(values, 0)))
+        sums = [0.0, 0.0]
+        for h in range(HEADS):
+            raw = dot_t(queries[h][:rows], keys)
+            weights = (jnp.exp2(raw) * mask).astype(BF)
+            count = jnp.where(lane_head == h + 1 - 2 * (h % 2), one, zero)
+            sums[h % 2] += dot(weights, jnp.where(lane_head == h, value, count))
         return sums
 
     def finished(sum_a, sum_b, tok):
@@ -409,7 +406,9 @@
     cattn = jnp.sum(cattn, 0, keepdims=True)
     loads["outc"].wait()
     cattn = jnp.broadcast_to(cattn, (HEADS_C, CC)).astype(BF)
-    result = coarse_f + dot(cattn, outc_v[...])
+    result = coarse_f
+    for first in range(0, CC, C):
+        result = result + dot(cattn[:, first : first + C], outc_v[first : first + C, :])
     coarse_o[...] = result[0:1].astype(BF)
 
     for copy in (halos, rows, tiles):

time: 28.8 us -> 28.8 us (level)
  no operation moved by 1% of the time
where the time goes in v5:
time: 28.8 us; the launch traced here: 28.7 us
  Pallas kernels  28.1 us (98%)
  between operations  0.64 us (2%)
    pallas_call x1, Pallas kernels, shards(): pl.pallas_call(functools.partial(kernel, sizes), out_shape=(pltpu.VMEM((C...  27.4 us
    pallas_call x1, Pallas kernels, shards(): pl.pallas_call(finish, out_shape=(jax.ShapeDtypeStruct((COUNT, C), BF), j...  0.68 us

profile of v5, /device:TPU:1, one launch (start us, length us, event | category | flops | bytes accessed | tf_op | source)
XLA Modules:
  0.0 28.7 jit_solution(9605051474977835282)
XLA Ops:
  0.6 27.4 %shard_map.167 = (bf16[256,256]{1,0:T(8,128)(2,1)S(1)}, bf16[1,1024]{1,0:T(2,128)(2,1)S(1)}) custom-call(bf16[256,256]{1,0:T(8,128)(2,1)} %bitcast.6, f32[1,256]{1,0:T(1,128)} %bitcast.8, bf16[256,768]{1,0:T(8,128)(2,1)} %qkv_fine.1, f32[4]{0:T(128)} %scale_fine.1, bf16[256,256]{1,0:T(8,128)(2,1)} %out_fine.1, f32[1,256]{1,0:T(1,128)} %bitcast.9, ...), custom_call_target="tpu_custom_call" | custom-call | tf_op jit(solution)/shard_map/pallas_call | solution.py:452
  28.1 0.7 %shard_map.168 = (bf16[256,256]{1,0:T(8,128)(2,1)}, bf16[1,1024]{1,0:T(2,128)(2,1)}) custom-call(bf16[256,256]{1,0:T(8,128)(2,1)S(1)} %get-tuple-element.6.fine, bf16[1,1024]{1,0:T(2,128)(2,1)S(1)} %get-tuple-element.7.coarse), custom_call_target="tpu_custom_call" | custom-call | tf_op jit(solution)/shard_map/pallas_call | solution.py:511

commit v6 on v5

--- a/solution.py
+++ b/solution.py
@@ -148,8 +148,8 @@
     n_ha, n_wa = sizes
     n_x, n_z = n_ha // 4, n_wa // 2
     g_row, g_tile = n_z * 2, n_x * 4
-    names = ("tok", "ga", "qkv", "pick", "table", "place", "sf", "out", "gf", "fin", "fout")
-    names += ("up", "gc", "sc", "qkvc", "outc")
+    names = ("tok", "ga", "qkv", "pick", "table", "place", "sf", "sc", "out", "gf", "fin", "fout")
+    again = ("up", "gc", "qkvc", "outc")
     pairs = {
         "tok": (tokens, tok_v),
         "ga": (gain_attn, ga_v),
@@ -169,7 +169,7 @@
         "outc": (out_coarse, outc_v),
     }
     loads = {}
-    for i, name in enumerate(names):
+    for i, name in list(enumerate(names)) + list(enumerate(again)):
         loads[name] = pltpu.make_async_copy(*pairs[name], local_sem.at[i])
     for name in names[:4]:
         loads[name].start()
@@ -237,6 +237,8 @@
     loads["qkv"].wait()
     proj = dot(normed, qkv_v[...])
     loads["pick"].wait()
+    for name in again:
+        loads[name].start()
     same = pick_v[:, COUNT:]
 
     def head_norm(values):
@@ -484,7 +486,7 @@
                 pltpu.VMEM((g_row, 1, C + LANES), F32),
                 pltpu.VMEM((g_row, C + LANES), BF),
                 pltpu.VMEM((g_tile, g_row, C + LANES), BF),
-                pltpu.SemaphoreType.DMA((16,)),
+                pltpu.SemaphoreType.DMA((12,)),
                 *[pltpu.SemaphoreType.DMA] * 6,
             ],
             compiler_params=pltpu.CompilerParams(

time: 28.8 us -> 28.8 us (level)
  no operation moved by 1% of the time
where the time goes in v6:
time: 28.8 us; the launch traced here: 28.7 us
  Pallas kernels  28.1 us (98%)
  between operations  0.64 us (2%)
    pallas_call x1, Pallas kernels, shards(): pl.pallas_call(functools.partial(kernel, sizes), out_shape=(pltpu.VMEM((C...  27.4 us
    pallas_call x1, Pallas kernels, shards(): pl.pallas_call(finish, out_shape=(jax.ShapeDtypeStruct((COUNT, C), BF), j...  0.68 us

profile of v6, /device:TPU:1, one launch (start us, length us, event | category | flops | bytes accessed | tf_op | source)
XLA Modules:
  0.0 28.7 jit_solution(7860954213047651495)
XLA Ops:
  0.6 27.4 %shard_map.167 = (bf16[256,256]{1,0:T(8,128)(2,1)S(1)}, bf16[1,1024]{1,0:T(2,128)(2,1)S(1)}) custom-call(bf16[256,256]{1,0:T(8,128)(2,1)} %bitcast.6, f32[1,256]{1,0:T(1,128)} %bitcast.8, bf16[256,768]{1,0:T(8,128)(2,1)} %qkv_fine.1, f32[4]{0:T(128)} %scale_fine.1, bf16[256,256]{1,0:T(8,128)(2,1)} %out_fine.1, f32[1,256]{1,0:T(1,128)} %bitcast.9, ...), custom_call_target="tpu_custom_call" | custom-call | tf_op jit(solution)/shard_map/pallas_call | solution.py:454
  28.0 0.7 %shard_map.168 = (bf16[256,256]{1,0:T(8,128)(2,1)}, bf16[1,1024]{1,0:T(2,128)(2,1)}) custom-call(bf16[256,256]{1,0:T(8,128)(2,1)S(1)} %get-tuple-element.6.fine, bf16[1,1024]{1,0:T(2,128)(2,1)S(1)} %get-tuple-element.7.coarse), custom_call_target="tpu_custom_call" | custom-call | tf_op jit(solution)/shard_map/pallas_call | solution.py:513
